TPU v7x, 512 devices: a whole 4x4x16 slice. The times are simulated.
512 devices in a mesh: dp: 8 (over x, z_hi), wide: 64 (over y, z_lo, core).
Axes of the slice: x: 4, y: 4, z: 16 (z_hi: 2, z_lo: 8; z = z_hi * 8 + z_lo), core: 2. Of those that a mesh axis runs over, the one named last changes fastest.
Arguments:
- latents: bfloat16 [8, 128, 8, 16, 256], P('dp', 'wide'), may hold values from -36 to 36
- cotangent: bfloat16 [8, 128, 8, 16, 256], P('dp', 'wide'), may hold values from -41 to 41
- norm_gain: float32 [256], replicated, may hold values from 0.25 to 1.75
- norm_bias: float32 [256], replicated, may hold values from -3 to 3
- w_spatial: bfloat16 [2304, 256], P('dp'), may hold values from -0.125 to 0.125
- w_temporal: bfloat16 [768, 256], P('dp'), may hold values from -0.21875 to 0.21875
Outputs:
- block_out: bfloat16 [8, 128, 8, 16, 256], P('dp', 'wide')
- grad_latents: bfloat16 [8, 128, 8, 16, 256], P('dp', 'wide')
- grad_spatial: float32 [2304, 256], P('dp', 'wide')
- grad_temporal: float32 [768, 256], P('dp', 'wide')
- grad_norm: float32 [2, 256], P(None, 'wide')
All inputs are finite; a program needn't handle non-finite values.
Results may differ from a plain program's by a relative error of at most 0.012.
Values may be sent and summed in bfloat16 or wider, within the bound.
A program may use at most 64 MiB of HBM per device.

v0:
```python
import math

import jax
import jax.numpy as jnp
from jax import lax
from jax.sharding import PartitionSpec as P

GROUPS = 32


epsilon = 1e-05


def contract(left, right):
    return lax.dot_general(
        left, right, (((0,), (0,)), ((), ())), preferred_element_type=jnp.float32
    )


def spatial_forward(activated, weights):
    frames, rows_here, cols_here, channels = activated.shape
    padded = jnp.pad(activated, ((0, 0), (1, 1), (1, 1), (0, 0)))
    running = jnp.zeros((frames * rows_here * cols_here, channels), jnp.float32)
    for tap_row in range(3):
        for tap_col in range(3):
            tap_index = 3 * tap_row + tap_col
            window = padded[
                :, tap_row : tap_row + rows_here, tap_col : tap_col + cols_here, :
            ].reshape(-1, channels)
            running = running + jnp.dot(
                window,
                weights[tap_index * channels : (tap_index + 1) * channels],
                preferred_element_type=jnp.float32,
            )
    return running.reshape(frames, rows_here, cols_here, channels)


def spatial_backward(activated, grad_out, weights):
    frames, rows_here, cols_here, channels = activated.shape
    pad_act = jnp.pad(activated, ((0, 0), (1, 1), (1, 1), (0, 0)))
    pad_grad = jnp.pad(grad_out, ((0, 0), (1, 1), (1, 1), (0, 0)))
    flat_grad = grad_out.reshape(-1, channels)
    running = jnp.zeros((frames * rows_here * cols_here, channels), jnp.float32)
    pieces = []
    for tap_row in range(3):
        for tap_col in range(3):
            tap_index = 3 * tap_row + tap_col
            block = weights[tap_index * channels : (tap_index + 1) * channels]
            window_grad = pad_grad[
                :, 2 - tap_row : 2 - tap_row + rows_here, 2 - tap_col : 2 - tap_col + cols_here, :
            ].reshape(-1, channels)
            running = running + jnp.dot(window_grad, block.T, preferred_element_type=jnp.float32)
            window_act = pad_act[
                :, tap_row : tap_row + rows_here, tap_col : tap_col + cols_here, :
            ].reshape(-1, channels)
            pieces.append(contract(window_act, flat_grad))
    return (
        running.reshape(frames, rows_here, cols_here, channels),
        jnp.concatenate(pieces, axis=0),
    )


def temporal_apply(extended, weights, frames):
    channels = extended.shape[-1]
    shape_out = (extended.shape[0], frames, extended.shape[2], channels)
    running = jnp.zeros((shape_out[0] * frames * shape_out[2], channels), jnp.float32)
    for time_delay in range(3):
        earlier = extended[:, 2 - time_delay : 2 - time_delay + frames].reshape(-1, channels)
        running = running + jnp.dot(
            earlier,
            weights[time_delay * channels : (time_delay + 1) * channels],
            preferred_element_type=jnp.float32,
        )
    return running.reshape(shape_out)


def temporal_adjoint(earlier_ext, later_ext, grad_rows, weights):
    frames = grad_rows.shape[1]
    channels = grad_rows.shape[-1]
    flat_grad = grad_rows.reshape(-1, channels)
    running = jnp.zeros(flat_grad.shape, jnp.float32)
    pieces = []
    for time_delay in range(3):
        block = weights[time_delay * channels : (time_delay + 1) * channels]
        later_rows = later_ext[:, time_delay : time_delay + frames].reshape(-1, channels)
        running = running + jnp.dot(later_rows, block.T, preferred_element_type=jnp.float32)
        earlier = earlier_ext[:, 2 - time_delay : 2 - time_delay + frames].reshape(-1, channels)
        pieces.append(contract(earlier, flat_grad))
    return (running.reshape(grad_rows.shape), jnp.concatenate(pieces, axis=0))


def local(latents, cotangent, norm_gain, norm_bias, w_spatial, w_temporal):
    clip_count, frames, rows_here, cols_here, channels = latents.shape
    per_group = channels // GROUPS
    cell_count = rows_here * cols_here
    spatial_full, temporal_full = (
        lax.all_gather(w_spatial, "dp", axis=0, tiled=True),
        lax.all_gather(w_temporal, "dp", axis=0, tiled=True),
    )
    widened = latents.astype(jnp.float32).reshape(
        clip_count, frames, rows_here, cols_here, GROUPS, per_group
    )
    group_sums = jnp.sum(widened, axis=(1, 2, 3, 5))
    squares = jnp.sum(widened * widened, axis=(1, 2, 3, 5))
    total_sums, total_squares = lax.psum((group_sums, squares), "wide")
    cells_count = lax.axis_size("wide") * frames * rows_here * cols_here * per_group
    group_mean = total_sums / cells_count
    variance = total_squares / cells_count - group_mean * group_mean
    inv_std = 1.0 / jnp.sqrt(variance + epsilon)
    mean_wide = group_mean[:, None, None, None, :, None]
    std_wide = inv_std[:, None, None, None, :, None]
    whitened = (widened - mean_wide) * std_wide
    flat_white = whitened.reshape(latents.shape)
    normed = flat_white * norm_gain + norm_bias
    sigmoid = jax.nn.sigmoid(normed)
    activated = (normed * sigmoid).astype(jnp.bfloat16)
    silu_slope = sigmoid * (1.0 + normed * (1.0 - sigmoid))
    stacked = activated.reshape(clip_count * frames, rows_here, cols_here, channels)
    spatial = (
        spatial_forward(stacked, spatial_full)
        .astype(jnp.bfloat16)
        .reshape(clip_count, frames, cell_count, channels)
    )
    grad_rows = cotangent.reshape(clip_count, frames, cell_count, channels)
    row_slab = lax.all_to_all(spatial, "wide", split_axis=2, concat_axis=1, tiled=True)
    extended = jnp.pad(row_slab, ((0, 0), (2, 0), (0, 0), (0, 0)))
    mixed_rows = temporal_apply(extended, temporal_full, row_slab.shape[1])
    returned = lax.all_to_all(
        mixed_rows.astype(jnp.bfloat16), "wide", split_axis=1, concat_axis=2, tiled=True
    ).astype(mixed_rows.dtype)
    grad_slab = lax.all_to_all(grad_rows, "wide", split_axis=2, concat_axis=1, tiled=True)
    earlier_ext = jnp.pad(row_slab, ((0, 0), (2, 0), (0, 0), (0, 0)))
    later_ext = jnp.pad(grad_slab, ((0, 0), (0, 2), (0, 0), (0, 0)))
    slab_wide, local_temporal = temporal_adjoint(earlier_ext, later_ext, grad_slab, temporal_full)
    grad_spatial_act = lax.all_to_all(
        slab_wide.astype(jnp.bfloat16), "wide", split_axis=1, concat_axis=2, tiled=True
    )
    block_out = (latents.astype(jnp.float32) + returned.reshape(latents.shape)).astype(jnp.bfloat16)
    grad_stack = grad_spatial_act.reshape(clip_count * frames, rows_here, cols_here, channels)
    grad_activated, local_spatial = spatial_backward(stacked, grad_stack, spatial_full)
    grad_normed = grad_activated.reshape(latents.shape) * silu_slope
    gain_term = jnp.sum(grad_normed * flat_white, axis=(0, 1, 2, 3))
    bias_term = jnp.sum(grad_normed, axis=(0, 1, 2, 3))
    local_norm = jnp.stack([gain_term, bias_term])
    grad_white = (grad_normed * norm_gain).reshape(widened.shape)
    mean_part = jnp.sum(grad_white, axis=(1, 2, 3, 5))
    cross_part = jnp.sum(grad_white * whitened, axis=(1, 2, 3, 5))
    mean_total, cross_total = lax.psum((mean_part, cross_part), "wide")
    grad_mean = mean_total / cells_count
    grad_cross = cross_total / cells_count
    inner = (
        grad_white
        - grad_mean[:, None, None, None, :, None]
        - whitened * grad_cross[:, None, None, None, :, None]
    ) * std_wide
    grad_latents = (cotangent.astype(jnp.float32) + inner.reshape(latents.shape)).astype(
        jnp.bfloat16
    )
    part_spatial, part_temporal, part_norm = (
        lax.psum_scatter(local_spatial, "wide", scatter_dimension=1, tiled=True),
        lax.psum_scatter(local_temporal, "wide", scatter_dimension=1, tiled=True),
        lax.psum_scatter(local_norm, "wide", scatter_dimension=1, tiled=True),
    )
    summed_spatial, summed_temporal = (
        lax.psum_scatter(
            part_spatial.astype(jnp.bfloat16), "dp", scatter_dimension=0, tiled=True
        ).astype(jnp.float32),
        lax.psum_scatter(
            part_temporal.astype(jnp.bfloat16), "dp", scatter_dimension=0, tiled=True
        ).astype(jnp.float32),
    )
    summed_norm = lax.psum(part_norm, "dp")
    all_cells = (
        clip_count * lax.axis_size("dp") * frames * lax.axis_size("wide") * rows_here * cols_here
    )
    grad_scale = 1.0 / math.sqrt(all_cells)
    return (
        block_out,
        grad_latents,
        summed_spatial * grad_scale,
        summed_temporal * grad_scale,
        summed_norm * grad_scale,
    )


def solution(mesh):
    return jax.shard_map(
        local,
        mesh=mesh,
        in_specs=(
            P("dp", "wide", None, None, None),
            P("dp", "wide", None, None, None),
            P(),
            P(),
            P("dp", None),
            P("dp", None),
        ),
        out_specs=(
            P("dp", "wide", None, None, None),
            P("dp", "wide", None, None, None),
            P("dp", "wide"),
            P("dp", "wide"),
            P(None, "wide"),
        ),
        check_vma=False,
    )
```

profile of v0, /device:TPU:1, one launch (start us, length us, event | category | flops | bytes accessed | tf_op | source)
XLA Modules:
  0.0 1140.1 jit_solution(14482897674854768501)
XLA Ops:
  7.2 0.7 all-gather.2.cloned.1.call-update
  7.9 1.7 copy.53
  9.6 17.2 %all-to-all-start.2 = ((bf16[1,2,128,256]{3,1,0,2:T(2,128)(2,1)}), bf16[1,2,128,256]{3,1,0,2:T(2,128)(2,1)S(1)}, u32[]{:S(2)}, u32[]{:S(2)}) async-start(bf16[1,2,128,256]{3,1,0,2:T(2,128)(2,1)} %bitcast.21), calls=%async_computation.2 | async-start | bytes 262144 | tf_op jit(solution)/shard_map/all_to_all | solution.py:131
  26.8 73.0 %all_gather.7 = bf16[768,256]{1,0:T(8,128)(2,1)S(1)} all-gather(bf16[96,256]{1,0:T(8,128)(2,1)} %param.11), channel_id=1, replica_groups=mesh['dp'=8,'wide'=64] {'dp'}, dimensions={0}, use_global_device_ids=true | all-gather | bytes 442368 | tf_op jit(solution)/shard_map/all_gather | solution.py:98
  99.9 0.6 copy-done.4
  101.0 0.2 fusion.33
  101.2 0.2 convolution_add_fusion.9
  101.5 0.2 fusion.2
  101.7 0.7 convert_element_type.114
  102.4 38.8 %all-to-all-start.3 = ((bf16[1,128,2,256]{3,2,0,1:T(2,128)(2,1)}), bf16[1,128,2,256]{3,2,0,1:T(2,128)(2,1)S(1)}, u32[]{:S(2)}, u32[]{:S(2)}) async-start(bf16[1,128,2,256]{3,2,0,1:T(2,128)(2,1)} %bitcast.25), calls=%async_computation.3 | async-start | bytes 262144 | tf_op jit(solution)/shard_map/all_to_all | solution.py:135
  141.7 210.5 %all-reduce.8 = (f32[1,32]{1,0:T(1,128)S(1)}, f32[1,32]{1,0:T(1,128)S(1)}) all-reduce(f32[1,32]{1,0:T(1,128)S(1)} %bitcast.167, f32[1,32]{1,0:T(1,128)S(1)} %bitcast.166), channel_id=1, replica_groups=mesh['dp'=8,'wide'=64] {'wide'}, use_global_device_ids=true, to_apply=%region_5.6 | all-reduce | flops 64 | bytes 512 | tf_op jit(solution)/shard_map/psum | solution.py:105
  352.6 1.3 dynamic-slice
  354.8 0.8 pad_slice_fusion.12
  355.8 1.2 fusion.53
  357.1 1.1 convolution_add_fusion.7
  358.2 0.2 convolution_add_fusion.6
  358.4 0.2 convolution_add_fusion.5
  358.7 0.2 convolution_add_fusion.4
  358.9 0.2 convolution_add_fusion.3
  359.1 0.2 convolution_add_fusion.2
  359.4 0.2 convolution_add_fusion.1
  359.6 0.2 convolution_add_fusion
  359.8 0.8 fusion.24
  360.7 0.6 reduce_sum.104
  361.4 0.6 reduce_sum.100
  362.2 0.9 convolution_dynamic-update-slice_fusion.8
  363.3 0.2 convolution_add_fusion.19
  363.5 0.2 convolution_add_fusion.18
  363.8 0.2 convolution_add_fusion.16
  364.2 0.2 convolution_add_fusion.14
  364.6 0.2 fusion
  364.8 0.8 copy.47
  365.6 14.7 %all-to-all-start = ((bf16[1,2,128,256]{3,1,0,2:T(2,128)(2,1)}), bf16[1,2,128,256]{3,1,0,2:T(2,128)(2,1)S(1)}, u32[]{:S(2)}, u32[]{:S(2)}) async-start(bf16[1,2,128,256]{3,1,0,2:T(2,128)(2,1)} %copy.47), calls=%async_computation | async-start | bytes 262144 | tf_op jit(solution)/shard_map/all_to_all | solution.py:125
  380.3 0.9 convolution_dynamic-update-slice_fusion.7
  381.2 0.9 convolution_dynamic-update-slice_fusion.6
  382.1 0.9 convolution_dynamic-update-slice_fusion.5
  383.1 0.9 convolution_dynamic-update-slice_fusion.4
  384.0 0.9 convolution_dynamic-update-slice_fusion.3
  385.0 0.9 convolution_dynamic-update-slice_fusion.2
  385.9 0.9 convolution_dynamic-update-slice_fusion.1
  386.8 0.9 convolution_dynamic-update-slice_fusion
  387.8 7.2 all-to-all-done
  395.0 0.9 convolution_bitcast_fusion
  396.6 0.9 fusion.60
  397.6 0.2 convolution_add_fusion.11
  397.8 0.9 fusion.61
  398.7 0.8 fusion.1
  399.5 1.6 convert_element_type.106
  401.1 1.2 pad_maximum_fusion
  402.3 451.4 %all-reduce.10 = (f32[1,32]{1,0:T(1,128)}, f32[1,32]{1,0:T(1,128)}, bf16[2304,256]{1,0:T(8,128)(2,1)}, bf16[768,256]{1,0:T(8,128)(2,1)}, f32[2,256]{1,0:T(2,128)}) all-reduce(f32[1,32]{1,0:T(1,128)} %bitcast.164, f32[1,32]{1,0:T(1,128)} %bitcast.165, f32[2304,256]{1,0:T(8,128)S(1)} %copy-done.1, ...), channel_id=1, replica_groups=mesh['dp'=8,'wide'=64] {'wide'}, use_global_device_ids=true, to_apply=%region_11.12 | all-reduce | flops 787008 | bytes 4723200 | tf_op jit(solution)/shard_map/psum | solution.py:148
  853.7 0.8 constant_dynamic-slice_fusion
  854.5 15.3 %all-to-all-start.1 = ((bf16[1,128,2,256]{3,2,0,1:T(2,128)(2,1)}), bf16[1,128,2,256]{3,2,0,1:T(2,128)(2,1)S(1)}, u32[]{:S(2)}, u32[]{:S(2)}) async-start(bf16[1,128,2,256]{3,2,0,1:T(2,128)(2,1)} %bitcast.149), calls=%async_computation.1 | async-start | bytes 262144 | tf_op jit(solution)/shard_map/all_to_all | solution.py:128
  869.8 39.9 %psum.39 = f32[2,4]{1,0:T(2,128)S(1)} all-reduce(f32[2,4]{1,0:T(2,128)S(1)} %constant_dynamic-slice_fusion), channel_id=1, replica_groups=mesh['dp'=8,'wide'=64] {'dp'}, use_global_device_ids=true, to_apply=%region_19.20 | all-reduce | flops 8 | bytes 64 | tf_op jit(solution)/shard_map/psum | solution.py:172
  909.7 0.6 broadcast_multiply_fusion
  910.3 1.7 dynamic-slice_convert_fusion.1
  912.0 2.1 dynamic-slice_convert_fusion
  914.6 0.3 reduce-scatter.6.cloned.1.call-update
  914.9 105.9 %reduce-scatter.8.cloned.1.call-done = bf16[96,4]{1,0:T(8,128)(2,1)} async-done(((bf16[768,4]{1,0:T(8,128)(2,1)}), bf16[96,4]{1,0:T(8,128)(2,1)}) %reduce-scatter.8.cloned.1.call-update) | async-done | bytes 784 | tf_op jit(solution)/shard_map/reduce_scatter | solution.py:168
  1020.8 0.7 convert_multiply_fusion.2
  1021.5 0.7 copy.69
  1022.2 108.6 %reduce-scatter.6.cloned.1.call-done = bf16[288,4]{1,0:T(8,128)(2,1)} async-done(((bf16[2304,4]{1,0:T(8,128)(2,1)}), bf16[288,4]{1,0:T(8,128)(2,1)}) %reduce-scatter.6.cloned.1.call-update) | async-done | bytes 2320 | tf_op jit(solution)/shard_map/reduce_scatter | solution.py:165
  1130.8 0.9 convert_multiply_fusion.1
  1131.7 0.7 copy.68
  1132.7 0.8 fusion.23
  (81 shorter events, 4.2 us)
Async XLA Ops:
  7.2 348.7 %all-gather.2.cloned.1.call-start = ((), (), s32[]{:S(2)}) async-start(), calls=%async_computation.6 | async-start | bytes 1327104 | tf_op jit(solution)/shard_map/all_gather | solution.py:97
  9.6 90.3 %all-to-all-start.2 = ((bf16[1,2,128,256]{3,1,0,2:T(2,128)(2,1)}), bf16[1,2,128,256]{3,1,0,2:T(2,128)(2,1)S(1)}, u32[]{:S(2)}, u32[]{:S(2)}) async-start(bf16[1,2,128,256]{3,1,0,2:T(2,128)(2,1)} %bitcast.21), calls=%async_computation.2 | async-start | bytes 262144 | tf_op jit(solution)/shard_map/all_to_all | solution.py:131
  99.9 0.7 copy-start.4
  101.0 40.2 %copy-start.2 = (bf16[1,2,8,16,256]{4,3,2,1,0:T(8,128)(2,1)S(1)}, bf16[1,2,8,16,256]{4,3,2,1,0:T(8,128)(2,1)}, u32[]{:S(2)}) copy-start(bf16[1,2,8,16,256]{4,3,2,1,0:T(8,128)(2,1)} %param.6) | copy-start | bytes 393220
  102.4 252.1 %all-to-all-start.3 = ((bf16[1,128,2,256]{3,2,0,1:T(2,128)(2,1)}), bf16[1,128,2,256]{3,2,0,1:T(2,128)(2,1)S(1)}, u32[]{:S(2)}, u32[]{:S(2)}) async-start(bf16[1,128,2,256]{3,2,0,1:T(2,128)(2,1)} %bitcast.25), calls=%async_computation.3 | async-start | bytes 262144 | tf_op jit(solution)/shard_map/all_to_all | solution.py:135
  355.8 2.4 copy-start
  359.1 0.7 copy-start.6
  359.1 0.7 copy-start.9
  365.6 29.4 %all-to-all-start = ((bf16[1,2,128,256]{3,1,0,2:T(2,128)(2,1)}), bf16[1,2,128,256]{3,1,0,2:T(2,128)(2,1)S(1)}, u32[]{:S(2)}, u32[]{:S(2)}) async-start(bf16[1,2,128,256]{3,1,0,2:T(2,128)(2,1)} %copy.47), calls=%async_computation | async-start | bytes 262144 | tf_op jit(solution)/shard_map/all_to_all | solution.py:125
  384.0 3.8 copy-start.7
  384.0 3.8 copy-start.8
  384.0 10.9 copy-start.5
  398.7 3.6 copy-start.1
  853.7 60.5 %copy-start.10 = (f32[1,32]{1,0:T(1,128)S(1)}, f32[1,32]{1,0:T(1,128)}, u32[]{:S(2)}) copy-start(f32[1,32]{1,0:T(1,128)} %get-tuple-element.31) | copy-start | bytes 388
  853.7 60.5 %copy-start.11 = (f32[1,32]{1,0:T(1,128)S(1)}, f32[1,32]{1,0:T(1,128)}, u32[]{:S(2)}) copy-start(f32[1,32]{1,0:T(1,128)} %get-tuple-element.32) | copy-start | bytes 388
  854.5 277.9 %all-to-all-start.1 = ((bf16[1,128,2,256]{3,2,0,1:T(2,128)(2,1)}), bf16[1,128,2,256]{3,2,0,1:T(2,128)(2,1)S(1)}, u32[]{:S(2)}, u32[]{:S(2)}) async-start(bf16[1,128,2,256]{3,2,0,1:T(2,128)(2,1)} %bitcast.149), calls=%async_computation.1 | async-start | bytes 262144 | tf_op jit(solution)/shard_map/all_to_all | solution.py:128
  869.7 151.0 %reduce-scatter.8.cloned.1.call-start = ((), (), s32[]{:S(2)}) async-start(), calls=%async_computation.8 | async-start | bytes 221184 | tf_op jit(solution)/shard_map/reduce_scatter | solution.py:168
  914.2 216.6 %reduce-scatter.6.cloned.1.call-start = ((), (), s32[]{:S(2)}) async-start(), calls=%async_computation.7 | async-start | bytes 663552 | tf_op jit(solution)/shard_map/reduce_scatter | solution.py:165
  914.6 218.1 %copy-start.3 = (bf16[1,2,8,16,256]{4,3,2,1,0:T(8,128)(2,1)S(1)}, bf16[1,2,8,16,256]{4,3,2,1,0:T(8,128)(2,1)}, u32[]{:S(2)}) copy-start(bf16[1,2,8,16,256]{4,3,2,1,0:T(8,128)(2,1)} %param.7) | copy-start | bytes 393220
Sparse Core Ops, SparseCore 0:
  11.2 114.0 all-gather.1
  914.3 106.4 reduce-scatter.7
  1025.9 104.8 reduce-scatter.5
where the time goes:
time: 1140 us
  blocking collectives  775 us (68%)
  waiting for transfers between devices  223 us (20%)
  starting transfers between devices  86.1 us (8%)
  matrix products  18.6 us (2%)
  local copies, waits for them, and re-layouts  16.2 us (1%)
  between operations  15 us (1%)
    psum x1, blocking collectives, local(): mean_total, cross_total = lax.psum((mean_part, cross_part), 'wide')  451 us
    psum x1, blocking collectives, local(): total_sums, total_squares = lax.psum((group_sums, squares), 'wide')  211 us
    reduce_scatter x1, waiting for transfers between devices, local(): lax.psum_scatter(part_spatial.astype(jnp.bfloat16), 'dp', scatter_dimensi...  109 us
    reduce_scatter x1, waiting for transfers between devices, local(): lax.psum_scatter(part_temporal.astype(jnp.bfloat16), 'dp', scatter_dimens...  106 us
    all_gather x1, blocking collectives, local(): lax.all_gather(w_temporal, 'dp', axis=0, tiled=True)  73 us
    psum x1, blocking collectives, local(): summed_norm = lax.psum(part_norm, 'dp')  39.9 us
    all_to_all x1, starting transfers between devices, local(): lax.all_to_all(slab_wide.astype(jnp.bfloat16), 'wide', split_axis=1, conc...  38.8 us
  transfers between devices with their start and end apart: 7, of which 3 were waited for; matrix products, arithmetic and copies ran while one was open for 2% of the time, Pallas kernels for 0%

commit v1 on v0

v1 whole, which is shorter than its diff:
```python
import math

import jax
import jax.numpy as jnp
from jax import lax
from jax.experimental import pallas as pl
from jax.experimental.pallas import tpu as pltpu
from jax.sharding import PartitionSpec as P

MESH = pl.DeviceIdType.MESH
F32 = jnp.float32
BF16 = jnp.bfloat16
GROUPS = 32
EPSILON = 1e-05
C = 256
CELLS = 128
COLS = 16
ROWS = 256
NX, NZH, NY, NZL, NC = 4, 2, 4, 8, 2
S_TILE = (0, 4, 9, 13)
T_TILE = (0, 1, 3, 4)
WIN = 7 * 128
ZWIN = 5 * 128


def coords():
    dp, wide = lax.axis_index("dp"), lax.axis_index("wide")
    return (
        lax.div(dp, 2),
        lax.rem(dp, 2),
        lax.div(wide, 16),
        lax.rem(lax.div(wide, 2), 8),
        lax.rem(wide, 2),
    )


def device(x, zh, y, zl, c):
    return (x * 2 + zh, (y * 8 + zl) * 2 + c)


def remote(src, dst, send_sem, recv_sem, target):
    return pltpu.make_async_remote_copy(
        src_ref=src,
        dst_ref=dst,
        send_sem=send_sem,
        recv_sem=recv_sem,
        device_id=target,
        device_id_type=MESH,
    )


def greet(targets):
    barrier = pltpu.get_barrier_semaphore()
    for target in targets:
        pl.semaphore_signal(barrier, inc=1, device_id=target, device_id_type=MESH)
    return lambda: pl.semaphore_wait(barrier, len(targets))


def plane_peers(x, zh, y, zl, c):
    mine = y * 2 + c
    peers = []
    for k in range(1, 8):
        other = lax.rem(mine + k, 8)
        peers.append((other, device(x, zh, lax.div(other, 2), zl, lax.rem(other, 2))))
    return mine, peers


def line_peers(x, zh, y, zl, c):
    peers = []
    for k in range(1, 8):
        other = lax.rem(zl + k, 8)
        peers.append((other, device(x, zh, y, other, c)))
    return zl, peers


class Exchange:
    def __init__(self, slots, send_sem, recv_sem, mine, peers):
        self.copies = []
        self.arrivals = []
        for at, (other, target) in enumerate(peers):
            self.copies.append(
                remote(slots.at[mine], slots.at[mine], send_sem.at[at], recv_sem.at[mine], target)
            )
            self.arrivals.append(
                remote(slots.at[other], slots.at[other], send_sem.at[at], recv_sem.at[other], target)
            )

    def start(self):
        for copy in self.copies:
            copy.start()

    def arrive(self):
        for arrival in self.arrivals:
            arrival.wait_recv()

    def drain(self):
        for copy in self.copies:
            copy.wait_send()


def total(slots, count):
    result = slots[0]
    for k in range(1, count):
        result = result + slots[k]
    return result


def group_ones():
    row = lax.broadcasted_iota(jnp.int32, (C, C), 0)
    col = lax.broadcasted_iota(jnp.int32, (C, C), 1)
    return (lax.div(row, C // GROUPS) == lax.div(col, C // GROUPS)).astype(F32)


def group_totals(two_rows):
    padded = jnp.concatenate([two_rows, jnp.zeros((6, C), F32)], axis=0)
    return jnp.dot(
        padded, group_ones(), precision=lax.Precision.HIGHEST, preferred_element_type=F32
    )


def gather_kernel(
    lat, cot, ws, wt, weights, lat_prev, cot_next, stats,
    plane, line, local_sem, halo_send, halo_recv,
    plane_send, plane_recv, line_send, line_recv,
    x1_send, x1_recv, z_send, z_recv, x2_send, x2_recv,
    y_send, y_recv, c1_send, c1_recv, c2_send, c2_recv,
):
    x, zh, y, zl, c = coords()
    wide = lax.axis_index("wide")
    local_copies = [
        pltpu.make_async_copy(ws, weights.at[zh, x, pl.ds(0, 288)], local_sem.at[0]),
        pltpu.make_async_copy(wt, weights.at[zh, x, pl.ds(288, 96)], local_sem.at[1]),
    ]
    for copy in local_copies:
        copy.start()
    mine, in_plane = plane_peers(x, zh, y, zl, c)
    _, in_line = line_peers(x, zh, y, zl, c)
    after = (lax.axis_index("dp"), lax.rem(wide + 1, 64))
    before = (lax.axis_index("dp"), lax.rem(wide + 63, 64))
    others_x = [lax.rem(x + k, NX) for k in (1, 2, 3)]
    others_y = [lax.rem(y + k, NY) for k in (1, 2, 3)]
    to_x = [device(o, zh, y, zl, c) for o in others_x]
    to_y = [device(x, zh, o, zl, c) for o in others_y]
    to_z = device(x, 1 - zh, y, zl, c)
    to_c = device(x, zh, y, zl, 1 - c)
    arrived = greet(
        [p for _, p in in_plane] + [p for _, p in in_line] + [after, before] + to_x + [to_z]
    )

    wide_lat = lat[...].astype(F32)
    plane[mine, 0:1, :] = jnp.sum(wide_lat, axis=0, keepdims=True)
    plane[mine, 1:2, :] = jnp.sum(wide_lat * wide_lat, axis=0, keepdims=True)
    arrived()

    first = Exchange(plane, plane_send, plane_recv, mine, in_plane)
    first.start()
    for copy in local_copies:
        copy.wait()
    half = pl.multiple_of(c * 192, 16)
    piece = pl.multiple_of(c * 192 + y * 48, 16)
    z_copy = remote(
        weights.at[zh, x, pl.ds(piece, 48)], weights.at[zh, x, pl.ds(piece, 48)],
        z_send.at[0], z_recv.at[0], to_z,
    )
    z_copy.start()
    halo = [
        remote(lat, lat_prev, halo_send.at[0], halo_recv.at[0], after),
        remote(cot, cot_next, halo_send.at[1], halo_recv.at[1], before),
    ]
    for copy in halo:
        copy.start()
    x1 = [
        remote(
            weights.at[zh, x, pl.ds(half, 192)], weights.at[zh, x, pl.ds(half, 192)],
            x1_send.at[k], x1_recv.at[x], to_x[k],
        )
        for k in range(3)
    ]
    for copy in x1:
        copy.start()

    first.arrive()
    line[zl] = total(plane, 8)
    second = Exchange(line, line_send, line_recv, zl, in_line)
    second.start()

    remote(
        weights.at[1 - zh, x, pl.ds(piece, 48)], weights.at[1 - zh, x, pl.ds(piece, 48)],
        z_send.at[0], z_recv.at[0], to_z,
    ).wait_recv()
    x2 = [
        remote(
            weights.at[1 - zh, x, pl.ds(piece, 48)], weights.at[1 - zh, x, pl.ds(piece, 48)],
            x2_send.at[k], x2_recv.at[x], to_x[k],
        )
        for k in range(3)
    ]
    for copy in x2:
        copy.start()

    second.arrive()
    stats[...] = total(line, 8)

    for k in range(3):
        o = others_x[k]
        part = weights.at[1 - zh, o, pl.ds(piece, 48)]
        remote(part, part, x2_send.at[k], x2_recv.at[o], to_x[k]).wait_recv()
    spread = weights.at[1 - zh, :, pl.ds(piece, 48)]
    ys = [remote(spread, spread, y_send.at[k], y_recv.at[y], to_y[k]) for k in range(3)]
    for copy in ys:
        copy.start()
    c1 = []
    for k in range(3):
        o = others_x[k]
        part = weights.at[zh, o, pl.ds(half, 192)]
        remote(part, part, x1_send.at[k], x1_recv.at[o], to_x[k]).wait_recv()
        copy = remote(part, part, c1_send.at[k], c1_recv.at[k], to_c)
        copy.start()
        c1.append(copy)
    for k in range(3):
        o = others_y[k]
        their_piece = pl.multiple_of(c * 192 + o * 48, 16)
        part = weights.at[1 - zh, :, pl.ds(their_piece, 48)]
        remote(part, part, y_send.at[k], y_recv.at[o], to_y[k]).wait_recv()
    part = weights.at[1 - zh, :, pl.ds(half, 192)]
    c2 = remote(part, part, c2_send.at[0], c2_recv.at[0], to_c)
    c2.start()

    other_half = pl.multiple_of((1 - c) * 192, 16)
    for k in range(3):
        part = weights.at[zh, others_x[k], pl.ds(other_half, 192)]
        remote(part, part, c1_send.at[k], c1_recv.at[k], to_c).wait_recv()
    part = weights.at[1 - zh, :, pl.ds(other_half, 192)]
    remote(part, part, c2_send.at[0], c2_recv.at[0], to_c).wait_recv()
    for copy in halo:
        copy.wait_recv()
    first.drain()
    second.drain()
    for copy in halo + x1 + [z_copy] + x2 + ys + c1 + [c2]:
        copy.wait_send()


def gather(lat, cot, ws, wt):
    vmem = pl.BlockSpec(memory_space=pltpu.VMEM)
    dma = pltpu.SemaphoreType.DMA
    return pl.pallas_call(
        gather_kernel,
        name="gather",
        out_shape=(
            jax.ShapeDtypeStruct((NZH, NX, 384, C), BF16),
            jax.ShapeDtypeStruct((ROWS, C), BF16),
            jax.ShapeDtypeStruct((ROWS, C), BF16),
            jax.ShapeDtypeStruct((2, C), F32),
        ),
        in_specs=[vmem] * 4,
        out_specs=(vmem,) * 4,
        scratch_shapes=[
            pltpu.VMEM((8, 2, C), F32),
            pltpu.VMEM((8, 2, C), F32),
            dma((2,)), dma((2,)), dma((2,)),
            dma((7,)), dma((8,)), dma((7,)), dma((8,)),
            dma((3,)), dma((4,)), dma((1,)), dma((1,)), dma((3,)), dma((4,)),
            dma((3,)), dma((4,)), dma((3,)), dma((3,)), dma((1,)), dma((1,)),
        ],
        compiler_params=pltpu.CompilerParams(
            collective_id=1, has_side_effects=True, vmem_limit_bytes=32 << 20
        ),
    )(lat, cot, ws, wt)


def column_iota(rows):
    return lax.rem(lax.broadcasted_iota(jnp.int32, (rows, C), 0), COLS)


def shifted(values, step):
    rows = values.shape[0]
    if step == 0:
        return values.astype(BF16)
    col = column_iota(rows)
    moved = pltpu.roll(values, (rows - step) % rows, 0)
    edge = COLS - 1 if step == 1 else 0
    return jnp.where(col == edge, 0.0, moved).astype(BF16)


def fill_windows(target, values, sign):
    frames = values.shape[0] // CELLS
    for dx in range(3):
        cols = shifted(values, sign * (dx - 1))
        for dy in range(3):
            step = sign * (dy - 1)
            lanes = pl.ds((3 * dy + dx) * C, C)
            if step == 0:
                target[:, lanes] = cols
                continue
            for frame in range(frames):
                base = frame * CELLS
                if step == 1:
                    target[base : base + CELLS - COLS, lanes] = cols[base + COLS : base + CELLS]
                    target[base + CELLS - COLS : base + CELLS, lanes] = jnp.zeros((COLS, C), BF16)
                else:
                    target[base + COLS : base + CELLS, lanes] = cols[base : base + CELLS - COLS]
                    target[base : base + COLS, lanes] = jnp.zeros((COLS, C), BF16)


def permutation():
    row = lax.broadcasted_iota(jnp.int32, (C, C), 0)
    col = lax.broadcasted_iota(jnp.int32, (C, C), 1)
    j = lax.rem(row, 4)
    zl = lax.rem(lax.div(row, 4), 4) + 4 * lax.rem(lax.div(row, 64), 2)
    y = lax.rem(lax.div(row, 16), 4)
    c = lax.div(row, 128)
    return (col == y * 64 + zl * 8 + c * 4 + j).astype(F32).astype(BF16)


def times_transpose(left, right):
    return lax.dot_general(left, right, (((1,), (1,)), ((), ())), preferred_element_type=F32)


def block_kernel(
    lat, cot, lat_prev, cot_next, stats, gain, bias, weights,
    block_out, grads, norm_sums, grad_white, white, inverse,
    windows, spatial, mixed, adjoint, w_sp, w_tm,
):
    wide = lax.axis_index("wide")
    for d in range(8):
        w_sp[d * 288 : (d + 1) * 288, :] = weights[d % 2, d // 2, 0:288, :]
        w_tm[d * 96 : (d + 1) * 96, :] = weights[d % 2, d // 2, 288:384, :]
    sums = group_totals(stats[...]) / (FRAMES_CELLS * (C // GROUPS))
    mean = sums[0:1]
    inv = 1.0 / jnp.sqrt(sums[1:2] - mean * mean + EPSILON)
    inverse[...] = inv
    gains, biases = gain[...], bias[...]

    def normed_of(values):
        whitened = (values.astype(F32) - mean) * inv
        return whitened, whitened * gains + biases

    whitened, normed = normed_of(lat[...])
    white[...] = whitened
    sigmoid = jax.nn.sigmoid(normed)
    slope = sigmoid * (1.0 + normed * (1.0 - sigmoid))
    _, before = normed_of(lat_prev[...])
    fill_windows(windows.at[ROWS:, :], normed * sigmoid, 1)
    fill_windows(windows.at[:ROWS, :], before * jax.nn.sigmoid(before), 1)
    conv = jnp.dot(windows[...], w_sp[...], preferred_element_type=F32)
    spatial[ROWS:, :] = conv[ROWS:].astype(BF16)
    spatial[:ROWS, :] = jnp.where(wide > 0, conv[:ROWS], 0.0).astype(BF16)
    for delay in range(3):
        start = (2 - delay) * CELLS
        mixed[:, delay * C : (delay + 1) * C] = spatial[start : start + ROWS, :]
    temporal = jnp.dot(mixed[...], w_tm[...], preferred_element_type=F32)
    block_out[...] = (lat[...].astype(F32) + temporal).astype(BF16)

    later = jnp.where(wide < 63, cot_next[...].astype(F32), 0.0).astype(BF16)
    own = cot[...]
    shifts = (own, jnp.concatenate([own[CELLS:], later[:CELLS]], axis=0), later)
    running = jnp.zeros((ROWS, C), F32)
    for delay in range(3):
        running = running + times_transpose(shifts[delay], w_tm[delay * C : (delay + 1) * C, :])
    grad_act = running.astype(BF16)
    fill_windows(adjoint, grad_act.astype(F32), -1)
    running = jnp.zeros((ROWS, C), F32)
    for tap in range(9):
        lanes = slice(tap * C, (tap + 1) * C)
        running = running + times_transpose(adjoint[:, lanes], w_sp[lanes, :])
    grad_normed = running * slope
    norm_sums[0:1, :] = jnp.sum(grad_normed * whitened, axis=0, keepdims=True)
    norm_sums[1:2, :] = jnp.sum(grad_normed, axis=0, keepdims=True)
    grad_white[...] = grad_normed * gains

    order = permutation()
    act_t = times_transpose(order, grad_act).astype(BF16)
    cot_t = times_transpose(order, own).astype(BF16)
    grads[:, : 9 * C] = jnp.dot(
        act_t, windows[ROWS:, :], preferred_element_type=F32
    ).astype(BF16)
    grads[:, 9 * C :] = jnp.dot(cot_t, mixed[...], preferred_element_type=F32).astype(BF16)


FRAMES_CELLS = 128 * CELLS


def block(lat, cot, lat_prev, cot_next, stats, gain, bias, weights):
    vmem = pl.BlockSpec(memory_space=pltpu.VMEM)
    return pl.pallas_call(
        block_kernel,
        name="block",
        out_shape=(
            jax.ShapeDtypeStruct((ROWS, C), BF16),
            jax.ShapeDtypeStruct((C, 12 * C), BF16),
            jax.ShapeDtypeStruct((2, C), F32),
            jax.ShapeDtypeStruct((ROWS, C), F32),
            jax.ShapeDtypeStruct((ROWS, C), F32),
            jax.ShapeDtypeStruct((1, C), F32),
        ),
        in_specs=[vmem] * 8,
        out_specs=(vmem,) * 6,
        scratch_shapes=[
            pltpu.VMEM((2 * ROWS, 9 * C), BF16),
            pltpu.VMEM((2 * ROWS, C), BF16),
            pltpu.VMEM((ROWS, 3 * C), BF16),
            pltpu.VMEM((ROWS, 9 * C), BF16),
            pltpu.VMEM((9 * C, C), BF16),
            pltpu.VMEM((3 * C, C), BF16),
        ],
        compiler_params=pltpu.CompilerParams(vmem_limit_bytes=48 << 20),
    )(lat, cot, lat_prev, cot_next, stats, gain, bias, weights)


def windows_of(values, which):
    s, t = S_TILE[which] * 128, (18 + T_TILE[which]) * 128
    return values[:, s : s + 640], values[:, t : t + 256]


def reduce_kernel(
    grads, norm_sums, grad_white, white, inverse, gain, cot,
    grad_latents, grad_sums, grad_norm,
    plane, line, chips, core_in, a1, b1, a1_in, b1_in, a2, b2, a2_in, b2_in, z1, z_in,
    plane_send, plane_recv, line_send, line_recv, chip_send, chip_recv,
    core_send, core_recv, a1_send, a1_recv, b1_send, b1_recv,
    a2_send, a2_recv, b2_send, b2_recv, zs_send, zs_recv,
):
    x, zh, y, zl, c = coords()
    wide, dp = lax.axis_index("wide"), lax.axis_index("dp")
    mine, in_plane = plane_peers(x, zh, y, zl, c)
    _, in_line = line_peers(x, zh, y, zl, c)
    others_x = [lax.rem(x + k, NX) for k in (1, 2, 3)]
    others_y = [lax.rem(y + k, NY) for k in (1, 2, 3)]
    to_x = [device(o, zh, y, zl, c) for o in others_x]
    to_y = [device(x, zh, o, zl, c) for o in others_y]
    to_c = device(x, zh, y, zl, 1 - c)
    others_dp = [lax.rem(dp + k, 8) for k in range(1, 8)]
    to_dp = [(o, wide) for o in others_dp]
    at_z = zh * 8 + zl
    others_z = [lax.rem(at_z + k, 16) for k in range(1, 16)]
    to_z = [device(x, lax.div(o, 8), y, lax.rem(o, 8), c) for o in others_z]
    arrived = greet([p for _, p in in_plane] + to_dp + to_z)
    plane[mine] = norm_sums[...]
    arrived()

    away = pl.multiple_of((1 - c) * 128, 128)
    core = remote(grads.at[pl.ds(away, 128)], core_in, core_send.at[0], core_recv.at[0], to_c)
    first = Exchange(plane, plane_send, plane_recv, mine, in_plane)
    first.start()
    core.start()
    first.arrive()
    line[zl] = total(plane, 8)
    second = Exchange(line, line_send, line_recv, zl, in_line)
    second.start()

    core.wait_recv()
    for o in range(NY):
        rows = pl.ds(pl.multiple_of(c * 128 + o * 16, 16), 16)
        a1[o] = (
            grads[rows, :].astype(F32) + core_in[o * 16 : (o + 1) * 16, :].astype(F32)
        ).astype(BF16)
    step_a1 = [
        remote(a1.at[others_y[k]], a1_in.at[y], a1_send.at[k], a1_recv.at[y], to_y[k])
        for k in range(3)
    ]
    for copy in step_a1:
        copy.start()
    rows = pl.ds(pl.multiple_of(c * 128 + 64, 16), 64)
    for o in range(NX):
        s, t = S_TILE[o] * 128, (18 + T_TILE[o]) * 128
        for start, width, put in ((s, 640, 0), (t, 256, 640)):
            b1[o, :, put : put + width] = (
                grads[rows, start : start + width].astype(F32)
                + core_in[64:128, start : start + width].astype(F32)
            ).astype(BF16)
    step_b1 = [
        remote(b1.at[others_x[k]], b1_in.at[x], b1_send.at[k], b1_recv.at[x], to_x[k])
        for k in range(3)
    ]
    for copy in step_b1:
        copy.start()

    second.arrive()
    sums = total(line, 8)
    chips[dp] = sums
    step_dp = [
        remote(chips.at[dp], chips.at[dp], chip_send.at[k], chip_recv.at[dp], to_dp[k])
        for k in range(7)
    ]
    for copy in step_dp:
        copy.start()
    means = group_totals(sums * gain[...]) / (FRAMES_CELLS * (C // GROUPS))
    inner = (grad_white[...] - means[1:2] - white[...] * means[0:1]) * inverse[...]
    grad_latents[...] = (cot[...].astype(F32) + inner).astype(BF16)

    for k in range(3):
        o = others_y[k]
        remote(a1.at[o], a1_in.at[o], a1_send.at[k], a1_recv.at[o], to_y[k]).wait_recv()
    joined = a1[y].astype(F32)
    for k in range(3):
        joined = joined + a1_in[others_y[k]].astype(F32)
    joined = joined.astype(BF16)
    for o in range(NX):
        s, t = windows_of(joined, o)
        a2[o, :, 0:640] = s
        a2[o, :, 640:WIN] = t
    step_a2 = [
        remote(a2.at[others_x[k]], a2_in.at[x], a2_send.at[k], a2_recv.at[x], to_x[k])
        for k in range(3)
    ]
    for copy in step_a2:
        copy.start()
    for k in range(3):
        o = others_x[k]
        remote(b1.at[o], b1_in.at[o], b1_send.at[k], b1_recv.at[o], to_x[k]).wait_recv()
    joined = b1[x].astype(F32)
    for k in range(3):
        joined = joined + b1_in[others_x[k]].astype(F32)
    joined = joined.astype(BF16)
    for o in range(NY):
        b2[o] = joined[o * 16 : (o + 1) * 16, :]
    step_b2 = [
        remote(b2.at[others_y[k]], b2_in.at[y], b2_send.at[k], b2_recv.at[y], to_y[k])
        for k in range(3)
    ]
    for copy in step_b2:
        copy.start()

    for k in range(3):
        o = others_x[k]
        remote(a2.at[o], a2_in.at[o], a2_send.at[k], a2_recv.at[o], to_x[k]).wait_recv()
    half_a = a2[x].astype(F32)
    for k in range(3):
        half_a = half_a + a2_in[others_x[k]].astype(F32)
    for k in range(3):
        o = others_y[k]
        remote(b2.at[o], b2_in.at[o], b2_send.at[k], b2_recv.at[o], to_y[k]).wait_recv()
    half_b = b2[y].astype(F32)
    for k in range(3):
        half_b = half_b + b2_in[others_y[k]].astype(F32)
    for h, part in enumerate((half_a, half_b)):
        for q in range(4):
            four = part[q * 4 : (q + 1) * 4, :]
            for hi in range(NZH):
                z1[hi * 8 + h * 4 + q, :, 0:384] = four[:, hi * 256 : hi * 256 + 384].astype(z1.dtype)
                z1[hi * 8 + h * 4 + q, :, 384:ZWIN] = four[:, 640:WIN].astype(z1.dtype)
    step_z = [
        remote(z1.at[others_z[k]], z_in.at[at_z], zs_send.at[k], zs_recv.at[at_z], to_z[k])
        for k in range(15)
    ]
    for copy in step_z:
        copy.start()

    scale = 1.0 / math.sqrt(131072)
    for k in range(7):
        o = others_dp[k]
        remote(chips.at[o], chips.at[o], chip_send.at[k], chip_recv.at[o], to_dp[k]).wait_recv()
    grad_norm[...] = total(chips, 8) * scale
    for k in range(15):
        o = others_z[k]
        remote(z1.at[o], z_in.at[o], zs_send.at[k], zs_recv.at[o], to_z[k]).wait_recv()
    result = z1[at_z].astype(F32)
    for k in range(15):
        result = result + z_in[others_z[k]].astype(F32)
    grad_sums[...] = result * scale
    first.drain()
    second.drain()
    for copy in [core] + step_a1 + step_b1 + step_dp + step_a2 + step_b2 + step_z:
        copy.wait_send()


Z_TYPE = BF16


def reduce(grads, norm_sums, grad_white, white, inverse, gain, cot):
    vmem = pl.BlockSpec(memory_space=pltpu.VMEM)
    dma = pltpu.SemaphoreType.DMA
    return pl.pallas_call(
        reduce_kernel,
        name="reduce",
        out_shape=(
            jax.ShapeDtypeStruct((ROWS, C), BF16),
            jax.ShapeDtypeStruct((4, ZWIN), F32),
            jax.ShapeDtypeStruct((2, C), F32),
        ),
        in_specs=[vmem] * 7,
        out_specs=(vmem,) * 3,
        scratch_shapes=[
            pltpu.VMEM((8, 2, C), F32),
            pltpu.VMEM((8, 2, C), F32),
            pltpu.VMEM((8, 2, C), F32),
            pltpu.VMEM((128, 12 * C), BF16),
            pltpu.VMEM((NY, 16, 12 * C), BF16),
            pltpu.VMEM((NX, 64, WIN), BF16),
            pltpu.VMEM((NY, 16, 12 * C), BF16),
            pltpu.VMEM((NX, 64, WIN), BF16),
            pltpu.VMEM((NX, 16, WIN), BF16),
            pltpu.VMEM((NY, 16, WIN), BF16),
            pltpu.VMEM((NX, 16, WIN), BF16),
            pltpu.VMEM((NY, 16, WIN), BF16),
            pltpu.VMEM((16, 4, ZWIN), Z_TYPE),
            pltpu.VMEM((16, 4, ZWIN), Z_TYPE),
            dma((7,)), dma((8,)), dma((7,)), dma((8,)), dma((7,)), dma((8,)),
            dma((1,)), dma((1,)), dma((3,)), dma((4,)), dma((3,)), dma((4,)),
            dma((3,)), dma((4,)), dma((3,)), dma((4,)), dma((15,)), dma((16,)),
        ],
        compiler_params=pltpu.CompilerParams(
            collective_id=2, has_side_effects=True, vmem_limit_bytes=48 << 20
        ),
    )(grads, norm_sums, grad_white, white, inverse, gain, cot)


def local(latents, cotangent, norm_gain, norm_bias, w_spatial, w_temporal):
    lat, cot = latents.reshape(ROWS, C), cotangent.reshape(ROWS, C)
    gain, bias = norm_gain.reshape(1, C), norm_bias.reshape(1, C)
    weights, lat_prev, cot_next, stats = gather(lat, cot, w_spatial, w_temporal)
    block_out, grads, norm_sums, grad_white, white, inverse = block(
        lat, cot, lat_prev, cot_next, stats, gain, bias, weights
    )
    grad_latents, grad_sums, grad_norm = reduce(
        grads, norm_sums, grad_white, white, inverse, gain, cot
    )
    dp, wide = lax.axis_index("dp"), lax.axis_index("wide")
    odd, hi = lax.rem(lax.div(dp, 2), 2), lax.rem(dp, 2)
    spatial = lax.dynamic_slice(grad_sums[:, :384], (0, 64 * odd + 32 * hi), (4, 288))
    temporal = lax.dynamic_slice(grad_sums[:, 384:], (0, 64 * odd + 96 * hi), (4, 96))
    return (
        block_out.reshape(latents.shape),
        grad_latents.reshape(latents.shape),
        spatial.T,
        temporal.T,
        lax.dynamic_slice(grad_norm, (0, 4 * wide), (2, 4)),
    )


def solution(mesh):
    return jax.shard_map(
        local,
        mesh=mesh,
        in_specs=(
            P("dp", "wide", None, None, None),
            P("dp", "wide", None, None, None),
            P(),
            P(),
            P("dp", None),
            P("dp", None),
        ),
        out_specs=(
            P("dp", "wide", None, None, None),
            P("dp", "wide", None, None, None),
            P("dp", "wide"),
            P("dp", "wide"),
            P(None, "wide"),
        ),
        check_vma=False,
    )
```

time: 1140 us -> 81.2 us (0.07)
  blocking collectives: 775 us -> 0 us
  waiting for transfers between devices: 223 us -> 0 us
  starting transfers between devices: 86.1 us -> 0 us
  Pallas kernels: 0 us -> 70.9 us
  matrix products: 18.6 us -> 0 us
  between operations: 15 us -> 0.72 us
    psum x3 -> x0, blocking collectives: 702 us -> none  [the longest x1 451 us: local(): mean_total, cross_total = lax.psum((mean_part, cross_part), 'wide')]
    reduce_scatter x2 -> x0, waiting for transfers between devices: 214 us -> none  [the longest x1 109 us: local(): lax.psum_scatter(part_spatial.astype(jnp.bfloat16), 'dp', scatter_dimensi...]
    all_to_all x4 -> x0, starting transfers between devices: 85.9 us -> none  [the longest x1 38.8 us: local(): lax.all_to_all(slab_wide.astype(jnp.bfloat16), 'wide', split_axis=1, conc...]
    all_gather x1 -> x0, blocking collectives: 73 us -> none  [local(): lax.all_gather(w_temporal, 'dp', axis=0, tiled=True)]
    pallas_call x0 -> x3, Pallas kernels: none -> 70.9 us  [the longest x1 36.2 us: gather(): pl.pallas_call(gather_kernel, name='gather', out_shape=(jax.ShapeDtypeStr...]
    dot_general x36 -> x0, matrix products: 18.6 us -> none  [the longest x12 11.2 us: contract(): lax.dot_general(left, right, (((0,), (0,)), ((), ())), preferred_element_...]
  transfers between devices with their start and end apart: 7 -> 0, of which waited for: 3 -> 0; matrix products, arithmetic and copies ran while one was open for 2% -> 0% of each run, Pallas kernels for 0% -> 0%
where the time goes in v1:
time: 81.2 us; the launch traced here: 80.9 us
  Pallas kernels  70.9 us (87%)
  local copies, waits for them, and re-layouts  9.29 us (11%)
    pallas_call x1, Pallas kernels, gather(): pl.pallas_call(gather_kernel, name='gather', out_shape=(jax.ShapeDtypeStr...  36.2 us
    pallas_call x1, Pallas kernels, reduce(): pl.pallas_call(reduce_kernel, name='reduce', out_shape=(jax.ShapeDtypeStr...  31.3 us
    unnamed x19, local copies, waits for them, and re-layouts  7.33 us
    pallas_call x1, Pallas kernels, block(): pl.pallas_call(block_kernel, name='block', out_shape=(jax.ShapeDtypeStruc...  3.42 us

profile of v1, /device:TPU:1, one launch (start us, length us, event | category | flops | bytes accessed | tf_op | source)
XLA Modules:
  0.0 80.9 jit_solution(6173656742948967118)
XLA Ops:
  0.6 0.0 copy-start
  0.6 0.9 %copy-done = bf16[1,2,8,16,256]{4,3,2,1,0:T(8,128)(2,1)S(1)} copy-done((bf16[1,2,8,16,256]{4,3,2,1,0:T(8,128)(2,1)S(1)}, bf16[1,2,8,16,256]{4,3,2,1,0:T(8,128)(2,1)}, u32[]{:S(2)}) %copy-start) | copy-done | bytes 131096
  1.5 0.0 copy-start.3
  1.5 0.9 %copy-done.3 = bf16[1,2,8,16,256]{4,3,2,1,0:T(8,128)(2,1)S(1)} copy-done((bf16[1,2,8,16,256]{4,3,2,1,0:T(8,128)(2,1)S(1)}, bf16[1,2,8,16,256]{4,3,2,1,0:T(8,128)(2,1)}, u32[]{:S(2)}) %copy-start.3) | copy-done | bytes 131096
  2.4 0.0 copy-start.5
  2.4 0.9 %copy-done.5 = bf16[288,256]{1,0:T(8,128)(2,1)S(1)} copy-done((bf16[288,256]{1,0:T(8,128)(2,1)S(1)}, bf16[288,256]{1,0:T(8,128)(2,1)}, u32[]{:S(2)}) %copy-start.5) | copy-done | bytes 147480
  3.4 0.0 copy-start.6
  3.4 0.8 copy-done.6
  4.2 0.0 copy-start.2
  4.2 36.2 %gather.1 = (bf16[2,4,384,256]{3,2,1,0:T(8,128)(2,1)S(1)}, bf16[256,256]{1,0:T(8,128)(2,1)S(1)}, bf16[256,256]{1,0:T(8,128)(2,1)S(1)}, f32[2,256]{1,0:T(2,128)S(1)}) custom-call(bf16[256,256]{1,0:T(8,128)(2,1)S(1)} %bitcast.13, bf16[256,256]{1,0:T(8,128)(2,1)S(1)} %bitcast.10, bf16[288,256]{1,0:T(8,128)(2,1)S(1)} %copy-done.5, bf16[96,256]{1,0:T(8,128)(2,1)S(1)} %copy-done.6), custom_call_target="tpu_custom_call" | custom-call | tf_op jit(solution)/shard_map/gather/pallas_call | solution.py:246
  40.3 0.0 copy-start.1
  40.3 0.9 %copy-done.1 = bf16[1,2,8,16,256]{4,3,2,1,0:T(8,128)(2,1)S(1)} copy-done((bf16[1,2,8,16,256]{4,3,2,1,0:T(8,128)(2,1)S(1)}, bf16[1,2,8,16,256]{4,3,2,1,0:T(8,128)(2,1)}, u32[]{:S(2)}) %copy-start.1) | copy-done | bytes 131096
  41.2 0.0 copy-start.4
  41.2 0.9 %copy-done.4 = bf16[1,2,8,16,256]{4,3,2,1,0:T(8,128)(2,1)S(1)} copy-done((bf16[1,2,8,16,256]{4,3,2,1,0:T(8,128)(2,1)S(1)}, bf16[1,2,8,16,256]{4,3,2,1,0:T(8,128)(2,1)}, u32[]{:S(2)}) %copy-start.4) | copy-done | bytes 131096
  42.1 0.0 copy-start.7
  42.1 0.7 copy-done.7
  42.8 0.0 copy-start.8
  42.8 0.7 copy-done.8
  43.5 3.4 %block.1 = (bf16[256,256]{1,0:T(8,128)(2,1)}, bf16[256,3072]{1,0:T(8,128)(2,1)S(1)}, f32[2,256]{1,0:T(2,128)S(1)}, f32[256,256]{1,0:T(8,128)S(1)}, f32[256,256]{1,0:T(8,128)S(1)}, /*index=5*/f32[1,256]{1,0:T(1,128)S(1)}) custom-call(bf16[256,256]{1,0:T(8,128)(2,1)S(1)} %bitcast.14, bf16[256,256]{1,0:T(8,128)(2,1)S(1)} %bitcast.11, ...), custom_call_target="tpu_custom_call" | custom-call | tf_op jit(solution)/shard_map/block/pallas_call | solution.py:385
  46.9 0.0 copy-done.2
  46.9 31.3 %reduce.1 = (bf16[256,256]{1,0:T(8,128)(2,1)S(1)}, f32[4,640]{1,0:T(4,128)S(1)}, f32[2,256]{1,0:T(2,128)S(1)}) custom-call(bf16[256,3072]{1,0:T(8,128)(2,1)S(1)} %get-tuple-element.23.grads, f32[2,256]{1,0:T(2,128)S(1)} %get-tuple-element.24.norm_sums, f32[256,256]{1,0:T(8,128)S(1)} %get-tuple-element.25.grad_white, f32[256,256]{1,0:T(8,128)S(1)} %get-tuple-element.26.white, ...), custom_call_target="tpu_custom_call" | custom-call | tf_op jit(solution)/shard_map/reduce/pallas_call | solution.py:573
  78.3 0.7 dynamic-slice_bitcast_fusion.1
  78.9 0.7 dynamic-slice_bitcast_fusion
  79.6 0.6 constant_dynamic-slice_fusion
  80.2 0.7 copy.12
  (2 shorter events, 0.0 us)
Async XLA Ops:
  0.6 0.9 %copy-start = (bf16[1,2,8,16,256]{4,3,2,1,0:T(8,128)(2,1)S(1)}, bf16[1,2,8,16,256]{4,3,2,1,0:T(8,128)(2,1)}, u32[]{:S(2)}) copy-start(bf16[1,2,8,16,256]{4,3,2,1,0:T(8,128)(2,1)} %param.7) | copy-start | bytes 393220
  1.5 0.9 %copy-start.3 = (bf16[1,2,8,16,256]{4,3,2,1,0:T(8,128)(2,1)S(1)}, bf16[1,2,8,16,256]{4,3,2,1,0:T(8,128)(2,1)}, u32[]{:S(2)}) copy-start(bf16[1,2,8,16,256]{4,3,2,1,0:T(8,128)(2,1)} %param.6) | copy-start | bytes 393220
  2.4 0.9 %copy-start.5 = (bf16[288,256]{1,0:T(8,128)(2,1)S(1)}, bf16[288,256]{1,0:T(8,128)(2,1)}, u32[]{:S(2)}) copy-start(bf16[288,256]{1,0:T(8,128)(2,1)} %ws.1) | copy-start | bytes 442372
  3.4 0.8 copy-start.6
  4.2 42.8 %copy-start.2 = (bf16[1,2,8,16,256]{4,3,2,1,0:T(8,128)(2,1)S(1)}, bf16[1,2,8,16,256]{4,3,2,1,0:T(8,128)(2,1)}, u32[]{:S(2)}) copy-start(bf16[1,2,8,16,256]{4,3,2,1,0:T(8,128)(2,1)} %param.7) | copy-start | bytes 393220
  40.3 0.9 %copy-start.1 = (bf16[1,2,8,16,256]{4,3,2,1,0:T(8,128)(2,1)S(1)}, bf16[1,2,8,16,256]{4,3,2,1,0:T(8,128)(2,1)}, u32[]{:S(2)}) copy-start(bf16[1,2,8,16,256]{4,3,2,1,0:T(8,128)(2,1)} %param.7) | copy-start | bytes 393220
  41.2 0.9 %copy-start.4 = (bf16[1,2,8,16,256]{4,3,2,1,0:T(8,128)(2,1)S(1)}, bf16[1,2,8,16,256]{4,3,2,1,0:T(8,128)(2,1)}, u32[]{:S(2)}) copy-start(bf16[1,2,8,16,256]{4,3,2,1,0:T(8,128)(2,1)} %param.6) | copy-start | bytes 393220
  42.1 0.7 copy-start.7
  42.8 0.7 copy-start.8

commit v2 on v0

v2 whole, which is shorter than its diff:
```python
import math

import jax
import jax.numpy as jnp
from jax import lax
from jax.experimental import pallas as pl
from jax.experimental.pallas import tpu as pltpu
from jax.sharding import PartitionSpec as P

MESH = pl.DeviceIdType.MESH
F32 = jnp.float32
BF16 = jnp.bfloat16
GROUPS = 32
EPSILON = 1e-05
C = 256
CELLS = 128
COLS = 16
ROWS = 256
NX, NZH, NY, NZL, NC = 4, 2, 4, 8, 2
S_TILE = (0, 4, 9, 13)
T_TILE = (0, 1, 3, 4)
WIN = 7 * 128
ZWIN = 5 * 128


def coords():
    dp, wide = lax.axis_index("dp"), lax.axis_index("wide")
    return (
        lax.div(dp, 2),
        lax.rem(dp, 2),
        lax.div(wide, 16),
        lax.rem(lax.div(wide, 2), 8),
        lax.rem(wide, 2),
    )


def device(x, zh, y, zl, c):
    return (x * 2 + zh, (y * 8 + zl) * 2 + c)


def remote(src, dst, send_sem, recv_sem, target):
    return pltpu.make_async_remote_copy(
        src_ref=src,
        dst_ref=dst,
        send_sem=send_sem,
        recv_sem=recv_sem,
        device_id=target,
        device_id_type=MESH,
    )


def greet(targets):
    barrier = pltpu.get_barrier_semaphore()
    for target in targets:
        pl.semaphore_signal(barrier, inc=1, device_id=target, device_id_type=MESH)
    return lambda: pl.semaphore_wait(barrier, len(targets))


def plane_peers(x, zh, y, zl, c):
    mine = y * 2 + c
    peers = []
    for k in range(1, 8):
        other = lax.rem(mine + k, 8)
        peers.append((other, device(x, zh, lax.div(other, 2), zl, lax.rem(other, 2))))
    return mine, peers


def line_peers(x, zh, y, zl, c):
    peers = []
    for k in range(1, 8):
        other = lax.rem(zl + k, 8)
        peers.append((other, device(x, zh, y, other, c)))
    return zl, peers


def total(slots, count):
    result = slots[0]
    for k in range(1, count):
        result = result + slots[k]
    return result


def group_ones():
    row = lax.broadcasted_iota(jnp.int32, (C, C), 0)
    col = lax.broadcasted_iota(jnp.int32, (C, C), 1)
    return (lax.div(row, C // GROUPS) == lax.div(col, C // GROUPS)).astype(F32)


def group_totals(two_rows):
    padded = jnp.concatenate([two_rows, jnp.zeros((6, C), F32)], axis=0)
    return jnp.dot(
        padded, group_ones(), precision=lax.Precision.HIGHEST, preferred_element_type=F32
    )


def column_iota(rows):
    return lax.rem(lax.broadcasted_iota(jnp.int32, (rows, C), 0), COLS)


def shifted(values, step):
    rows = values.shape[0]
    if step == 0:
        return values.astype(BF16)
    col = column_iota(rows)
    moved = pltpu.roll(values, (rows - step) % rows, 0)
    edge = COLS - 1 if step == 1 else 0
    return jnp.where(col == edge, 0.0, moved).astype(BF16)


def fill_windows(target, values, sign):
    frames = values.shape[0] // CELLS
    for dx in range(3):
        cols = shifted(values, sign * (dx - 1))
        for dy in range(3):
            step = sign * (dy - 1)
            lanes = pl.ds((3 * dy + dx) * C, C)
            if step == 0:
                target[:, lanes] = cols
                continue
            for frame in range(frames):
                base = frame * CELLS
                if step == 1:
                    target[base : base + CELLS - COLS, lanes] = cols[base + COLS : base + CELLS]
                    target[base + CELLS - COLS : base + CELLS, lanes] = jnp.zeros((COLS, C), BF16)
                else:
                    target[base + COLS : base + CELLS, lanes] = cols[base : base + CELLS - COLS]
                    target[base : base + COLS, lanes] = jnp.zeros((COLS, C), BF16)


def permutation():
    row = lax.broadcasted_iota(jnp.int32, (C, C), 0)
    col = lax.broadcasted_iota(jnp.int32, (C, C), 1)
    j = lax.rem(row, 4)
    zl = lax.rem(lax.div(row, 4), 4) + 4 * lax.rem(lax.div(row, 64), 2)
    y = lax.rem(lax.div(row, 16), 4)
    c = lax.div(row, 128)
    return (col == y * 64 + zl * 8 + c * 4 + j).astype(F32).astype(BF16)


def times_transpose(left, right):
    return lax.dot_general(left, right, (((1,), (1,)), ((), ())), preferred_element_type=F32)


FRAMES_CELLS = 128 * CELLS


def windows_of(values, which):
    s, t = S_TILE[which] * 128, (18 + T_TILE[which]) * 128
    return values[:, s : s + 640], values[:, t : t + 256]


SENDS = 96
VMEM_BYTES = 62 << 20


def main_kernel(
    lat_hbm, cot_hbm, ws_hbm, wt_hbm, gain_hbm, bias_hbm,
    out_hbm, latents_hbm, sums_hbm, norm_hbm,
    block_out, grad_latents, grad_sums, grad_norm, lat, cot, gain, bias, lat_prev, cot_next, weights,
    plane, line, plane_b, line_b, pair_b, row_b,
    w_sp, w_tm, windows, spatial, mixed, adjoint, act_t, cot_t,
    away, own, core_in, a1, b1, a1_in, b1_in, a2, b2, a2_in, b2_in, z1, z_in,
    local_sem, store_sem, send_sem,
    plane_recv, line_recv, plane_b_recv, line_b_recv, pair_b_recv, row_b_recv,
    halo_recv, x1_recv, z_recv, x2_recv, y_recv, c1_recv, c2_recv,
    core_recv, a1_recv, b1_recv, a2_recv, b2_recv, zs_recv,
):
    x, zh, y, zl, c = coords()
    wide, dp = lax.axis_index("wide"), lax.axis_index("dp")
    loads = [
        pltpu.make_async_copy(source, target, local_sem.at[k])
        for k, (source, target) in enumerate(
            (
                (lat_hbm, lat),
                (ws_hbm, weights.at[zh, x, pl.ds(0, 288)]),
                (wt_hbm, weights.at[zh, x, pl.ds(288, 96)]),
                (cot_hbm, cot),
                (gain_hbm, gain),
                (bias_hbm, bias),
            )
        )
    ]
    for copy in loads:
        copy.start()
    mine, in_plane = plane_peers(x, zh, y, zl, c)
    _, in_line = line_peers(x, zh, y, zl, c)
    after = (dp, lax.rem(wide + 1, 64))
    before = (dp, lax.rem(wide + 63, 64))
    others_x = [lax.rem(x + k, NX) for k in (1, 2, 3)]
    others_y = [lax.rem(y + k, NY) for k in (1, 2, 3)]
    to_x = [device(o, zh, y, zl, c) for o in others_x]
    to_y = [device(x, zh, o, zl, c) for o in others_y]
    to_c = device(x, zh, y, zl, 1 - c)
    to_far = device(x, 1 - zh, y, lax.rem(zl + 4, 8), c)
    at_z = zh * 8 + zl
    others_z = [lax.rem(at_z + k, 16) for k in range(1, 16)]
    to_z = [device(x, lax.div(o, 8), y, lax.rem(o, 8), c) for o in others_z]
    arrived = greet([p for _, p in in_plane] + [after, before] + to_x + to_z)

    stores = []

    def store(source, target):
        copy = pltpu.make_async_copy(source, target, store_sem.at[len(stores)])
        copy.start()
        stores.append(copy)

    pending = []
    counter = [0]

    def send(source, target, recv, where):
        copy = remote(source, target, send_sem.at[counter[0]], recv, where)
        counter[0] += 1
        copy.start()
        pending.append(copy)

    def receive(ref, recv):
        remote(ref, ref, send_sem.at[0], recv, to_c).wait_recv()

    def exchange(slots, recv, at, peers):
        for _, target in peers:
            send(slots.at[at], slots.at[at], recv.at[at], target)

    def gathered(slots, recv, peers):
        for other, _ in peers:
            receive(slots.at[other], recv.at[other])

    loads[0].wait()
    wide_lat = lat[...].astype(F32)
    plane[mine, 0:1, :] = jnp.sum(wide_lat, axis=0, keepdims=True)
    plane[mine, 1:2, :] = jnp.sum(wide_lat * wide_lat, axis=0, keepdims=True)
    for copy in loads[1:]:
        copy.wait()
    arrived()

    exchange(plane, plane_recv, mine, in_plane)
    half = pl.multiple_of(c * 192, 16)
    other_half = pl.multiple_of((1 - c) * 192, 16)
    piece = pl.multiple_of(c * 192 + y * 48, 16)
    part = weights.at[zh, x, pl.ds(piece, 48)]
    send(part, part, z_recv.at[0], to_far)
    part = weights.at[zh, x, pl.ds(half, 192)]
    for target in to_x:
        send(part, part, x1_recv.at[x], target)
    send(lat, lat_prev, halo_recv.at[0], after)
    send(cot, cot_next, halo_recv.at[1], before)

    gathered(plane, plane_recv, in_plane)
    line[zl] = total(plane, 8)
    exchange(line, line_recv, zl, in_line)

    part = weights.at[1 - zh, x, pl.ds(piece, 48)]
    receive(part, z_recv.at[0])
    for target in to_x:
        send(part, part, x2_recv.at[x], target)
    for o in others_x:
        part = weights.at[zh, o, pl.ds(half, 192)]
        receive(part, x1_recv.at[o])
        send(part, part, c1_recv.at[o], to_c)
    for o in others_x:
        receive(weights.at[1 - zh, o, pl.ds(piece, 48)], x2_recv.at[o])
    part = weights.at[1 - zh, :, pl.ds(piece, 48)]
    for target in to_y:
        send(part, part, y_recv.at[y], target)

    gathered(line, line_recv, in_line)
    sums = group_totals(total(line, 8)) / (FRAMES_CELLS * (C // GROUPS))
    mean = sums[0:1]
    inv = 1.0 / jnp.sqrt(sums[1:2] - mean * mean + EPSILON)
    gains, biases = gain[...], bias[...]

    def normed_of(values):
        whitened = (values.astype(F32) - mean) * inv
        return whitened, whitened * gains + biases

    whitened, normed = normed_of(lat[...])
    fill_windows(windows.at[ROWS:, :], normed * jax.nn.sigmoid(normed), 1)
    receive(lat_prev, halo_recv.at[0])
    _, earlier = normed_of(lat_prev[...])
    fill_windows(windows.at[:ROWS, :], earlier * jax.nn.sigmoid(earlier), 1)
    order = permutation()
    cot_t[...] = times_transpose(order, cot[...]).astype(BF16)

    for o in others_y:
        their_piece = pl.multiple_of(c * 192 + o * 48, 16)
        receive(weights.at[1 - zh, :, pl.ds(their_piece, 48)], y_recv.at[o])
    part = weights.at[1 - zh, :, pl.ds(half, 192)]
    send(part, part, c2_recv.at[0], to_c)
    receive(cot_next, halo_recv.at[1])
    for o in others_x:
        receive(weights.at[zh, o, pl.ds(other_half, 192)], c1_recv.at[o])
    receive(weights.at[1 - zh, :, pl.ds(other_half, 192)], c2_recv.at[0])

    for d in range(8):
        w_sp[d * 288 : (d + 1) * 288, :] = weights[d % 2, d // 2, 0:288, :]
        w_tm[d * 96 : (d + 1) * 96, :] = weights[d % 2, d // 2, 288:384, :]

    later = jnp.where(wide < 63, cot_next[...].astype(F32), 0.0).astype(BF16)
    held = cot[...]
    shifts = (held, jnp.concatenate([held[CELLS:], later[:CELLS]], axis=0), later)
    running = jnp.zeros((ROWS, C), F32)
    for delay in range(3):
        running = running + times_transpose(shifts[delay], w_tm[delay * C : (delay + 1) * C, :])
    grad_act = running.astype(BF16)
    act_t[...] = times_transpose(order, grad_act).astype(BF16)

    theirs = pl.ds(pl.multiple_of((1 - c) * 128, 128), 128)
    ours = pl.ds(pl.multiple_of(c * 128, 128), 128)
    away[0:128, : 9 * C] = jnp.dot(
        act_t[theirs, :], windows[ROWS:, :], preferred_element_type=F32
    ).astype(BF16)
    send(away.at[:, pl.ds(0, 9 * C)], core_in.at[:, pl.ds(0, 9 * C)], core_recv.at[0], to_c)

    conv = jnp.dot(windows[...], w_sp[...], preferred_element_type=F32)
    spatial[ROWS:, :] = conv[ROWS:].astype(BF16)
    spatial[:ROWS, :] = jnp.where(wide > 0, conv[:ROWS], 0.0).astype(BF16)
    for delay in range(3):
        start = (2 - delay) * CELLS
        mixed[:, delay * C : (delay + 1) * C] = spatial[start : start + ROWS, :]
    away[:, 9 * C :] = jnp.dot(
        cot_t[theirs, :], mixed[...], preferred_element_type=F32
    ).astype(BF16)
    send(away.at[:, pl.ds(9 * C, 3 * C)], core_in.at[:, pl.ds(9 * C, 3 * C)], core_recv.at[1], to_c)

    own[:, : 9 * C] = jnp.dot(act_t[ours, :], windows[ROWS:, :], preferred_element_type=F32)
    own[:, 9 * C :] = jnp.dot(cot_t[ours, :], mixed[...], preferred_element_type=F32)

    receive(core_in.at[:, pl.ds(0, 9 * C)], core_recv.at[0])
    receive(core_in.at[:, pl.ds(9 * C, 3 * C)], core_recv.at[1])
    for o in range(NY):
        rows = slice(o * 16, (o + 1) * 16)
        a1[o] = (own[rows, :] + core_in[rows, :].astype(F32)).astype(BF16)
    for o, target in zip(others_y, to_y):
        send(a1.at[o], a1_in.at[y], a1_recv.at[y], target)
    for o in range(NX):
        s, t = S_TILE[o] * 128, (18 + T_TILE[o]) * 128
        for start, width, put in ((s, 640, 0), (t, 256, 640)):
            lanes = slice(start, start + width)
            b1[o, :, put : put + width] = (
                own[64:128, lanes] + core_in[64:128, lanes].astype(F32)
            ).astype(BF16)
    for o, target in zip(others_x, to_x):
        send(b1.at[o], b1_in.at[x], b1_recv.at[x], target)

    fill_windows(adjoint, grad_act.astype(F32), -1)
    running = jnp.zeros((ROWS, C), F32)
    for tap in range(9):
        lanes = slice(tap * C, (tap + 1) * C)
        running = running + times_transpose(adjoint[:, lanes], w_sp[lanes, :])
    sigmoid = jax.nn.sigmoid(normed)
    grad_normed = running * (sigmoid * (1.0 + normed * (1.0 - sigmoid)))
    plane_b[mine, 0:1, :] = jnp.sum(grad_normed * whitened, axis=0, keepdims=True)
    plane_b[mine, 1:2, :] = jnp.sum(grad_normed, axis=0, keepdims=True)
    exchange(plane_b, plane_b_recv, mine, in_plane)
    grad_white = grad_normed * gains

    temporal = jnp.dot(mixed[...], w_tm[...], preferred_element_type=F32)
    block_out[...] = (lat[...].astype(F32) + temporal).astype(BF16)
    store(block_out, out_hbm)

    gathered(plane_b, plane_b_recv, in_plane)
    line_b[zl] = total(plane_b, 8)
    exchange(line_b, line_b_recv, zl, in_line)

    for o in others_y:
        receive(a1_in.at[o], a1_recv.at[o])
    joined = a1[y].astype(F32)
    for o in others_y:
        joined = joined + a1_in[o].astype(F32)
    joined = joined.astype(BF16)
    for o in range(NX):
        s, t = windows_of(joined, o)
        a2[o, :, 0:640] = s
        a2[o, :, 640:WIN] = t
    for o, target in zip(others_x, to_x):
        send(a2.at[o], a2_in.at[x], a2_recv.at[x], target)
    for o in others_x:
        receive(b1_in.at[o], b1_recv.at[o])
    joined = b1[x].astype(F32)
    for o in others_x:
        joined = joined + b1_in[o].astype(F32)
    joined = joined.astype(BF16)
    for o in range(NY):
        b2[o] = joined[o * 16 : (o + 1) * 16, :]
    for o, target in zip(others_y, to_y):
        send(b2.at[o], b2_in.at[y], b2_recv.at[y], target)

    for o in others_x:
        receive(a2_in.at[o], a2_recv.at[o])
    half_a = a2[x].astype(F32)
    for o in others_x:
        half_a = half_a + a2_in[o].astype(F32)
    for o in others_y:
        receive(b2_in.at[o], b2_recv.at[o])
    half_b = b2[y].astype(F32)
    for o in others_y:
        half_b = half_b + b2_in[o].astype(F32)
    for h, part in enumerate((half_a, half_b)):
        for q in range(4):
            four = part[q * 4 : (q + 1) * 4, :]
            for hi in range(NZH):
                z1[hi * 8 + h * 4 + q, :, 0:384] = four[:, hi * 256 : hi * 256 + 384].astype(BF16)
                z1[hi * 8 + h * 4 + q, :, 384:ZWIN] = four[:, 640:WIN].astype(BF16)
    for o, target in zip(others_z, to_z):
        send(z1.at[o], z_in.at[at_z], zs_recv.at[at_z], target)

    gathered(line_b, line_b_recv, in_line)
    sums_b = total(line_b, 8)
    pair_b[zh] = sums_b
    send(pair_b.at[zh], pair_b.at[zh], pair_b_recv.at[zh], to_far)
    means = group_totals(sums_b * gains) / (FRAMES_CELLS * (C // GROUPS))
    inner = (grad_white - means[1:2] - whitened * means[0:1]) * inv
    grad_latents[...] = (cot[...].astype(F32) + inner).astype(BF16)
    store(grad_latents, latents_hbm)
    receive(pair_b.at[1 - zh], pair_b_recv.at[1 - zh])
    row_b[x] = pair_b[0] + pair_b[1]
    for target in to_x:
        send(row_b.at[x], row_b.at[x], row_b_recv.at[x], target)

    scale = 1.0 / math.sqrt(131072)
    for o in others_z:
        receive(z_in.at[o], zs_recv.at[o])
    result = z1[at_z].astype(F32)
    for o in others_z:
        result = result + z_in[o].astype(F32)
    grad_sums[...] = result * scale
    store(grad_sums, sums_hbm)
    for o in others_x:
        receive(row_b.at[o], row_b_recv.at[o])
    grad_norm[...] = total(row_b, 4) * scale
    store(grad_norm, norm_hbm)
    for copy in stores:
        copy.wait()
    for copy in pending:
        copy.wait_send()


def main(lat, cot, ws, wt, gain, bias):
    hbm = pl.BlockSpec(memory_space=pltpu.HBM)
    dma = pltpu.SemaphoreType.DMA
    V = pltpu.VMEM
    return pl.pallas_call(
        main_kernel,
        name="main",
        out_shape=(
            jax.ShapeDtypeStruct((ROWS, C), BF16),
            jax.ShapeDtypeStruct((ROWS, C), BF16),
            jax.ShapeDtypeStruct((4, ZWIN), F32),
            jax.ShapeDtypeStruct((2, C), F32),
        ),
        in_specs=[hbm] * 6,
        out_specs=(hbm,) * 4,
        scratch_shapes=[
            V((ROWS, C), BF16), V((ROWS, C), BF16), V((4, ZWIN), F32), V((2, C), F32),
            V((ROWS, C), BF16), V((ROWS, C), BF16), V((1, C), F32), V((1, C), F32),
            V((ROWS, C), BF16), V((ROWS, C), BF16), V((NZH, NX, 384, C), BF16),
            V((8, 2, C), F32), V((8, 2, C), F32), V((8, 2, C), F32), V((8, 2, C), F32),
            V((NZH, 2, C), F32), V((NX, 2, C), F32),
            V((9 * C, C), BF16), V((3 * C, C), BF16),
            V((2 * ROWS, 9 * C), BF16), V((2 * ROWS, C), BF16), V((ROWS, 3 * C), BF16),
            V((ROWS, 9 * C), BF16), V((C, ROWS), BF16), V((C, ROWS), BF16),
            V((128, 12 * C), BF16), V((128, 12 * C), F32), V((128, 12 * C), BF16),
            V((NY, 16, 12 * C), BF16), V((NX, 64, WIN), BF16),
            V((NY, 16, 12 * C), BF16), V((NX, 64, WIN), BF16),
            V((NX, 16, WIN), BF16), V((NY, 16, WIN), BF16),
            V((NX, 16, WIN), BF16), V((NY, 16, WIN), BF16),
            V((16, 4, ZWIN), BF16), V((16, 4, ZWIN), BF16),
            dma((6,)), dma((4,)), dma((SENDS,)),
            dma((8,)), dma((8,)), dma((8,)), dma((8,)), dma((2,)), dma((4,)),
            dma((2,)), dma((4,)), dma((1,)), dma((4,)), dma((4,)), dma((4,)), dma((1,)),
            dma((2,)), dma((4,)), dma((4,)), dma((4,)), dma((4,)), dma((16,)),
        ],
        compiler_params=pltpu.CompilerParams(
            collective_id=1, has_side_effects=True, vmem_limit_bytes=VMEM_BYTES
        ),
    )(lat, cot, ws, wt, gain, bias)


def finish_kernel(
    main_out, main_latents, main_sums, main_norms,
    out_hbm, latents_hbm, spatial_hbm, temporal_hbm, norm_hbm,
    sums, norms, block_out, grad_latents, spatial, temporal, norm, load_sem, store_sem,
):
    dp, wide = lax.axis_index("dp"), lax.axis_index("wide")
    copies = [
        pltpu.make_async_copy(main_sums, sums, load_sem.at[0]),
        pltpu.make_async_copy(main_norms, norms, load_sem.at[1]),
        pltpu.make_async_copy(main_out, block_out, load_sem.at[2]),
        pltpu.make_async_copy(main_latents, grad_latents, load_sem.at[3]),
    ]
    for copy in copies:
        copy.start()
    copies[0].wait()
    odd, hi = lax.rem(lax.div(dp, 2), 2), lax.rem(dp, 2)
    pick_s, pick_t = jnp.zeros((4, 288), F32), jnp.zeros((4, 96), F32)
    for at_odd in range(2):
        for at_hi in range(2):
            here = jnp.logical_and(odd == at_odd, hi == at_hi)
            s, t = 64 * at_odd + 32 * at_hi, 384 + 64 * at_odd + 96 * at_hi
            pick_s = jnp.where(here, sums[:, s : s + 288], pick_s)
            pick_t = jnp.where(here, sums[:, t : t + 96], pick_t)
    spatial[...] = pick_s
    temporal[...] = pick_t
    copies[1].wait()
    lane = lax.broadcasted_iota(jnp.int32, (2, C), 1)
    for k in range(4):
        norm[:, k : k + 1] = jnp.sum(
            jnp.where(lane == 4 * wide + k, norms[...], 0.0), axis=1, keepdims=True
        )
    copies[2].wait()
    copies[3].wait()
    stores = [
        pltpu.make_async_copy(source, target, store_sem.at[k])
        for k, (source, target) in enumerate(
            (
                (block_out, out_hbm),
                (grad_latents, latents_hbm),
                (spatial, spatial_hbm),
                (temporal, temporal_hbm),
                (norm, norm_hbm),
            )
        )
    ]
    for copy in stores:
        copy.start()
    for copy in stores:
        copy.wait()


def finish(*parts):
    hbm = pl.BlockSpec(memory_space=pltpu.HBM)
    dma = pltpu.SemaphoreType.DMA
    outs = [((ROWS, C), BF16), ((ROWS, C), BF16), ((4, 288), F32), ((4, 96), F32), ((2, 4), F32)]
    return pl.pallas_call(
        finish_kernel,
        name="finish",
        out_shape=[jax.ShapeDtypeStruct(*shape) for shape in outs],
        in_specs=[hbm] * 4,
        out_specs=[hbm] * 5,
        scratch_shapes=[pltpu.VMEM((4, ZWIN), F32), pltpu.VMEM((2, C), F32)]
        + [pltpu.VMEM(*shape) for shape in outs]
        + [dma((4,)), dma((5,))],
        compiler_params=pltpu.CompilerParams(vmem_limit_bytes=VMEM_BYTES),
    )(*parts)


def local(latents, cotangent, norm_gain, norm_bias, w_spatial, w_temporal):
    block_out, grad_latents, spatial, temporal, norm = finish(
        *main(
            latents.reshape(ROWS, C),
            cotangent.reshape(ROWS, C),
            w_spatial,
            w_temporal,
            norm_gain.reshape(1, C),
            norm_bias.reshape(1, C),
        )
    )
    return (
        block_out.reshape(latents.shape),
        grad_latents.reshape(latents.shape),
        spatial.T,
        temporal.T,
        norm,
    )


def solution(mesh):
    return jax.shard_map(
        local,
        mesh=mesh,
        in_specs=(
            P("dp", "wide", None, None, None),
            P("dp", "wide", None, None, None),
            P(),
            P(),
            P("dp", None),
            P("dp", None),
        ),
        out_specs=(
            P("dp", "wide", None, None, None),
            P("dp", "wide", None, None, None),
            P("dp", "wide"),
            P("dp", "wide"),
            P(None, "wide"),
        ),
        check_vma=False,
    )
```

time: 1140 us -> 62.7 us (0.06)
  the two profiles are of different devices: /device:TPU:1 before, /device:TPU:2 now
where the time goes in v2:
time: 62.7 us; the launch traced here: 62.5 us
  Pallas kernels  61.9 us (99%)
  between operations  0.64 us (1%)
    pallas_call x1, Pallas kernels, main(): pl.pallas_call(main_kernel, name='main', out_shape=(jax.ShapeDtypeStruct(...  60 us
    pallas_call x1, Pallas kernels, finish(): pl.pallas_call(finish_kernel, name='finish', out_shape=[jax.ShapeDtypeStr...  1.86 us

profile of v2, /device:TPU:2, one launch (start us, length us, event | category | flops | bytes accessed | tf_op | source)
XLA Modules:
  0.0 62.5 jit_solution(9931226165751102704)
XLA Ops:
  0.6 60.0 %main.1 = (bf16[256,256]{1,0:T(8,128)(2,1)}, bf16[256,256]{1,0:T(8,128)(2,1)}, f32[4,640]{1,0:T(4,128)}, f32[2,256]{1,0:T(2,128)}) custom-call(bf16[256,256]{1,0:T(8,128)(2,1)} %bitcast.8, bf16[256,256]{1,0:T(8,128)(2,1)} %bitcast.9, bf16[288,256]{1,0:T(8,128)(2,1)} %ws_hbm.1, bf16[96,256]{1,0:T(8,128)(2,1)} %wt_hbm.1, f32[1,256]{1,0:T(1,128)} %bitcast.10, ...), custom_call_target="tpu_custom_call" | custom-call | tf_op jit(solution)/shard_map/main/pallas_call | solution.py:441
  60.7 1.9 %finish.1 = (bf16[256,256]{1,0:T(8,128)(2,1)}, bf16[256,256]{1,0:T(8,128)(2,1)}, f32[4,288]{1,0:T(4,128)}, f32[4,96]{1,0:T(4,128)}, f32[2,4]{1,0:T(2,128)}) custom-call(bf16[256,256]{1,0:T(8,128)(2,1)} %get-tuple-element.14.main_out, bf16[256,256]{1,0:T(8,128)(2,1)} %get-tuple-element.15.main_latents, f32[4,640]{1,0:T(4,128)} %get-tuple-element.16.main_sums, ...), custom_call_target="tpu_custom_call" | custom-call | tf_op jit(solution)/shard_map/finish/pallas_call | solution.py:533

commit v3 on v2

v3 whole, which is shorter than its diff:
```python
import math

import jax
import jax.numpy as jnp
from jax import lax
from jax.experimental import pallas as pl
from jax.experimental.pallas import tpu as pltpu
from jax.sharding import PartitionSpec as P

MESH = pl.DeviceIdType.MESH
F32 = jnp.float32
BF16 = jnp.bfloat16
GROUPS = 32
EPSILON = 1e-05
C = 256
CELLS = 128
COLS = 16
ROWS = 256
NX, NZH, NY, NZL, NC = 4, 2, 4, 8, 2
S_TILE = (0, 4, 9, 13)
T_TILE = (0, 1, 3, 4)
S_WIN = 5 * 128
T_WIN = 2 * 128
HALF = 128


def coords():
    dp, wide = lax.axis_index("dp"), lax.axis_index("wide")
    return (
        lax.div(dp, 2),
        lax.rem(dp, 2),
        lax.div(wide, 16),
        lax.rem(lax.div(wide, 2), 8),
        lax.rem(wide, 2),
    )


def device(x, zh, y, zl, c):
    return (x * 2 + zh, (y * 8 + zl) * 2 + c)


def remote(src, dst, send_sem, recv_sem, target):
    return pltpu.make_async_remote_copy(
        src_ref=src,
        dst_ref=dst,
        send_sem=send_sem,
        recv_sem=recv_sem,
        device_id=target,
        device_id_type=MESH,
    )


def greet(targets):
    barrier = pltpu.get_barrier_semaphore()
    for target in targets:
        pl.semaphore_signal(barrier, inc=1, device_id=target, device_id_type=MESH)
    return lambda: pl.semaphore_wait(barrier, len(targets))


def plane_peers(x, zh, y, zl, c):
    mine = y * 2 + c
    peers = []
    for k in range(1, 8):
        other = lax.rem(mine + k, 8)
        peers.append((other, device(x, zh, lax.div(other, 2), zl, lax.rem(other, 2))))
    return mine, peers


def line_peers(x, zh, y, zl, c):
    peers = []
    for k in range(1, 8):
        other = lax.rem(zl + k, 8)
        peers.append((other, device(x, zh, y, other, c)))
    return zl, peers


def total(slots, count):
    result = slots[0]
    for k in range(1, count):
        result = result + slots[k]
    return result


def group_ones():
    row = lax.broadcasted_iota(jnp.int32, (C, C), 0)
    col = lax.broadcasted_iota(jnp.int32, (C, C), 1)
    return (lax.div(row, C // GROUPS) == lax.div(col, C // GROUPS)).astype(F32)


def group_totals(two_rows):
    padded = jnp.concatenate([two_rows, jnp.zeros((6, C), F32)], axis=0)
    return jnp.dot(
        padded, group_ones(), precision=lax.Precision.HIGHEST, preferred_element_type=F32
    )


def column_iota(rows):
    return lax.rem(lax.broadcasted_iota(jnp.int32, (rows, C), 0), COLS)


def shifted(values, step):
    rows = values.shape[0]
    if step == 0:
        return values.astype(BF16)
    col = column_iota(rows)
    moved = pltpu.roll(values, (rows - step) % rows, 0)
    edge = COLS - 1 if step == 1 else 0
    return jnp.where(col == edge, 0.0, moved).astype(BF16)


def fill_windows(target, values, sign):
    frames = values.shape[0] // CELLS
    for dx in range(3):
        cols = shifted(values, sign * (dx - 1))
        for dy in range(3):
            step = sign * (dy - 1)
            lanes = pl.ds((3 * dy + dx) * C, C)
            if step == 0:
                target[:, lanes] = cols
                continue
            for frame in range(frames):
                base = frame * CELLS
                if step == 1:
                    target[base : base + CELLS - COLS, lanes] = cols[base + COLS : base + CELLS]
                    target[base + CELLS - COLS : base + CELLS, lanes] = jnp.zeros((COLS, C), BF16)
                else:
                    target[base + COLS : base + CELLS, lanes] = cols[base : base + CELLS - COLS]
                    target[base : base + COLS, lanes] = jnp.zeros((COLS, C), BF16)


def permutation(c):
    row = lax.broadcasted_iota(jnp.int32, (HALF, C), 0)
    col = lax.broadcasted_iota(jnp.int32, (HALF, C), 1)
    y, zl, j = lax.div(row, 32), lax.rem(lax.div(row, 4), 8), lax.rem(row, 4)
    return (col == y * 64 + zl * 8 + c * 4 + j).astype(F32).astype(BF16)


def times_transpose(left, right):
    return lax.dot_general(left, right, (((1,), (1,)), ((), ())), preferred_element_type=F32)


FRAMES_CELLS = 128 * CELLS


SENDS = 160
VMEM_BYTES = 62 << 20


def main_kernel(
    lat_hbm, cot_hbm, ws_hbm, wt_hbm, gain_hbm, bias_hbm,
    out_hbm, latents_hbm, s_hbm, t_hbm, norm_hbm,
    block_out, grad_latents, s_out, t_out, norm_out,
    frames, gain, bias, wsp, wtm,
    plane, line, plane_b, line_b, row_b, deep_b,
    w_sp, w_tm, windows, spatial, mixed, grad_act, adjoint, cot_t,
    s1, s1_in, t1, t1_in, zs, zs_in, zt, zt_in,
    local_sem, store_sem, send_sem,
    plane_recv, line_recv, plane_b_recv, line_b_recv, row_b_recv, deep_b_recv,
    mate_recv, halo_recv, pass_recv, tx_recv, tz_recv, txy_recv,
    sx_recv, sz_recv, sxy_recv, c1_recv, c2_recv, s1_recv, t1_recv, zs_recv, zt_recv,
):
    x, zh, y, zl, c = coords()
    wide, dp = lax.axis_index("wide"), lax.axis_index("dp")
    lat_at, cot_at, edge_out, edge_in = 1 + c, 3 + c, 3 - c, 5 - 5 * c
    lat, cot = frames.at[lat_at], frames.at[cot_at]
    loads = [
        pltpu.make_async_copy(source, target, local_sem.at[k])
        for k, (source, target) in enumerate(
            (
                (lat_hbm, lat),
                (wt_hbm, wtm.at[zh, x]),
                (ws_hbm, wsp.at[zh, x]),
                (cot_hbm, cot),
                (gain_hbm, gain),
                (bias_hbm, bias),
            )
        )
    ]
    for copy in loads:
        copy.start()
    mine, in_plane = plane_peers(x, zh, y, zl, c)
    _, in_line = line_peers(x, zh, y, zl, c)
    others_x = [lax.rem(x + k, NX) for k in (1, 2, 3)]
    to_x = [device(o, zh, y, zl, c) for o in others_x]
    to_c = device(x, zh, y, zl, 1 - c)
    to_far = device(x, 1 - zh, y, lax.rem(zl + 4, 8), c)
    ahead, behind = (dp, lax.rem(wide + 2, 64)), (dp, lax.rem(wide + 62, 64))
    edge_to = (dp, lax.rem(wide + 62 + 4 * c, 64))
    at_xy = x * 4 + y
    in_xy = []
    for k in range(1, 16):
        ox, oy = lax.rem(x + k // 4, NX), lax.rem(y + k % 4, NY)
        in_xy.append((ox * 4 + oy, device(ox, zh, oy, zl, c), ox, oy))
    at_z = zh * 8 + zl
    in_z = []
    for k in range(1, 16):
        o = lax.rem(at_z + k, 16)
        in_z.append((o, device(x, lax.div(o, 8), y, lax.rem(o, 8), c)))
    arrived = greet(
        [p for _, p in in_plane]
        + [p for _, p in in_line]
        + [in_xy[k - 1][1] for k in range(4, 16)]
        + [to_far, ahead, behind]
    )

    stores = []

    def store(source, target):
        copy = pltpu.make_async_copy(source, target, store_sem.at[len(stores)])
        copy.start()
        stores.append(copy)

    pending = []

    def send(ref, target, recv, where):
        copy = remote(ref, target, send_sem.at[len(pending)], recv, where)
        copy.start()
        pending.append(copy)

    def receive(ref, recv):
        remote(ref, ref, send_sem.at[0], recv, to_c).wait_recv()

    def exchange(slots, recv, at, peers):
        for _, target in peers:
            send(slots.at[at], slots.at[at], recv.at[at], target)

    def gathered(slots, recv, peers):
        for other, _ in peers:
            receive(slots.at[other], recv.at[other])

    loads[0].wait()
    wide_lat = lat[...].astype(F32)
    plane[mine, 0:1, :] = jnp.sum(wide_lat, axis=0, keepdims=True)
    plane[mine, 1:2, :] = jnp.sum(wide_lat * wide_lat, axis=0, keepdims=True)
    for copy in loads[1:]:
        copy.wait()
    arrived()

    exchange(plane, plane_recv, mine, in_plane)
    lanes = pl.ds(pl.multiple_of(c * HALF, HALF), HALF)
    t_rows = pl.ds(y * 3, 3)
    s_rows = pl.ds(y * 9, 9)
    part = wtm.at[zh, x, t_rows]
    send(part, part, tz_recv.at[0], to_far)
    part = wsp.at[zh, x, s_rows, :, lanes]
    send(part, part, sz_recv.at[0], to_far)
    for target in to_x:
        send(wtm.at[zh, x], wtm.at[zh, x], tx_recv.at[x], target)
    send(lat, lat, mate_recv.at[0], to_c)
    send(cot, cot, mate_recv.at[1], to_c)
    send(frames.at[edge_out], frames.at[edge_in], halo_recv.at[0], edge_to)
    part = wsp.at[zh, x, :, :, lanes]
    for target in to_x:
        send(part, part, sx_recv.at[x], target)

    gathered(plane, plane_recv, in_plane)
    line[zl] = total(plane, 8)
    exchange(line, line_recv, zl, in_line)

    part = wtm.at[1 - zh, x, t_rows]
    receive(part, tz_recv.at[0])
    for _, target, _, _ in in_xy:
        send(part, part, txy_recv.at[at_xy], target)
    part = wsp.at[1 - zh, x, s_rows, :, lanes]
    receive(part, sz_recv.at[0])
    for _, target, _, _ in in_xy:
        send(part, part, sxy_recv.at[at_xy], target)
    receive(frames.at[edge_in], halo_recv.at[0])
    send(frames.at[edge_in], frames.at[edge_in], pass_recv.at[0], to_c)
    for o in others_x:
        part = wsp.at[zh, o, :, :, lanes]
        receive(part, sx_recv.at[o])
        send(part, part, c1_recv.at[o], to_c)
    receive(frames.at[2 - c], mate_recv.at[0])
    receive(frames.at[4 - c], mate_recv.at[1])
    order = permutation(c)
    for k in range(2):
        cot_t[:, k * ROWS : (k + 1) * ROWS] = times_transpose(order, frames[3 + k]).astype(BF16)

    gathered(line, line_recv, in_line)
    sums = group_totals(total(line, 8)) / (FRAMES_CELLS * (C // GROUPS))
    mean = sums[0:1]
    inv = 1.0 / jnp.sqrt(sums[1:2] - mean * mean + EPSILON)
    gains, biases = gain[...], bias[...]

    def normed_of(values):
        whitened = (values.astype(F32) - mean) * inv
        return whitened, whitened * gains + biases

    for k in (1, 2):
        _, normed = normed_of(frames[k])
        fill_windows(
            windows.at[k * ROWS : (k + 1) * ROWS, :], normed * jax.nn.sigmoid(normed), 1
        )

    receive(frames.at[5 * c], pass_recv.at[0])
    last = frames[5]
    later = jnp.where(wide < 62, last.astype(F32), 0.0).astype(BF16)
    for o in others_x:
        receive(wtm.at[zh, o], tx_recv.at[o])
    for slot, _, ox, oy in in_xy:
        receive(wtm.at[1 - zh, ox, pl.ds(oy * 3, 3)], txy_recv.at[slot])
    for d in range(8):
        w_tm[d * 96 : (d + 1) * 96, :] = wtm[d % 2, d // 2].reshape(96, C)
    held = jnp.concatenate([frames[3], frames[4], later], axis=0)
    running = jnp.zeros((2 * ROWS, C), F32)
    for delay in range(3):
        start = delay * CELLS
        running = running + times_transpose(
            held[start : start + 2 * ROWS], w_tm[delay * C : (delay + 1) * C, :]
        )
    grad_act[...] = running.astype(BF16)
    act_t = times_transpose(order, grad_act[...]).astype(BF16)
    for o in range(NX):
        start = S_TILE[o] * 128
        piece = jnp.dot(
            act_t, windows[ROWS:, start : start + S_WIN], preferred_element_type=F32
        ).astype(BF16)
        for p in range(NY):
            s1[o * 4 + p] = piece[p * 32 : (p + 1) * 32, :]
    for slot, target, _, _ in in_xy:
        send(s1.at[slot], s1_in.at[at_xy], s1_recv.at[at_xy], target)

    own_rows = pl.ds(pl.multiple_of(c * ROWS, ROWS), ROWS)
    fill_windows(adjoint, grad_act[own_rows, :].astype(F32), -1)
    _, normed = normed_of(frames[0])
    fill_windows(windows.at[0:ROWS, :], normed * jax.nn.sigmoid(normed), 1)

    for slot, _, ox, oy in in_xy:
        receive(wsp.at[1 - zh, ox, pl.ds(oy * 9, 9), :, lanes], sxy_recv.at[slot])
    part = wsp.at[1 - zh, :, :, :, lanes]
    send(part, part, c2_recv.at[0], to_c)
    other_lanes = pl.ds(pl.multiple_of((1 - c) * HALF, HALF), HALF)
    for o in others_x:
        receive(wsp.at[zh, o, :, :, other_lanes], c1_recv.at[o])
    receive(wsp.at[1 - zh, :, :, :, other_lanes], c2_recv.at[0])
    for d in range(8):
        w_sp[d * 288 : (d + 1) * 288, :] = wsp[d % 2, d // 2].reshape(288, C)

    running = jnp.zeros((ROWS, C), F32)
    for tap in range(9):
        taps = slice(tap * C, (tap + 1) * C)
        running = running + times_transpose(adjoint[:, taps], w_sp[taps, :])
    whitened, normed = normed_of(lat[...])
    sigmoid = jax.nn.sigmoid(normed)
    grad_normed = running * (sigmoid * (1.0 + normed * (1.0 - sigmoid)))
    plane_b[mine, 0:1, :] = jnp.sum(grad_normed * whitened, axis=0, keepdims=True)
    plane_b[mine, 1:2, :] = jnp.sum(grad_normed, axis=0, keepdims=True)
    exchange(plane_b, plane_b_recv, mine, in_plane)
    grad_white = grad_normed * gains

    conv = jnp.dot(windows[...], w_sp[...], preferred_element_type=F32)
    spatial[ROWS:, :] = conv[ROWS:].astype(BF16)
    spatial[:ROWS, :] = jnp.where(wide > 1, conv[:ROWS], 0.0).astype(BF16)
    for delay in range(3):
        start = (2 - delay) * CELLS
        mixed[:, delay * C : (delay + 1) * C] = spatial[start : start + 2 * ROWS, :]
    for o in range(NX):
        start = T_TILE[o] * 128
        piece = jnp.dot(
            cot_t[...], mixed[:, start : start + T_WIN], preferred_element_type=F32
        ).astype(BF16)
        for p in range(NY):
            t1[o * 4 + p] = piece[p * 32 : (p + 1) * 32, :]
    for slot, target, _, _ in in_xy:
        send(t1.at[slot], t1_in.at[at_xy], t1_recv.at[at_xy], target)
    temporal = jnp.dot(mixed[own_rows, :], w_tm[...], preferred_element_type=F32)
    block_out[...] = (lat[...].astype(F32) + temporal).astype(BF16)
    store(block_out, out_hbm)

    gathered(plane_b, plane_b_recv, in_plane)
    sums_b = total(plane_b, 8)
    line_b[zl] = sums_b
    row_b[x] = sums_b
    exchange(line_b, line_b_recv, zl, in_line)
    for target in to_x:
        send(row_b.at[x], row_b.at[x], row_b_recv.at[x], target)

    odd = lax.rem(x, 2)

    def across_z(slots, slots_in, recv, source, source_in, source_recv, width):
        for slot, _, _, _ in in_xy:
            receive(source_in.at[slot], source_recv.at[slot])
        joined = source[at_xy].astype(F32)
        for slot, _, _, _ in in_xy:
            joined = joined + source_in[slot].astype(F32)
        for hi in range(NZH):
            at = width * hi
            mid = jnp.where(
                odd == 1, joined[:, at + 64 : at + 64 + width], joined[:, at : at + width]
            )
            for q in range(8):
                slots[hi * 8 + q, :, 0:width] = mid[q * 4 : (q + 1) * 4].astype(BF16)
                slots[hi * 8 + q, :, width:] = jnp.zeros((4, slots.shape[2] - width), BF16)
        for o, target in in_z:
            send(slots.at[o], slots_in.at[at_z], recv.at[at_z], target)

    scale = 1.0 / math.sqrt(131072)

    def at_last(slots, slots_in, recv, out, out_hbm):
        for o, _ in in_z:
            receive(slots_in.at[o], recv.at[o])
        result = slots[at_z].astype(F32)
        for o, _ in in_z:
            result = result + slots_in[o].astype(F32)
        out[...] = result * scale
        store(out, out_hbm)

    across_z(zs, zs_in, zs_recv, s1, s1_in, s1_recv, 288)
    for o in others_x:
        receive(row_b.at[o], row_b_recv.at[o])
    deep_b[at_z] = total(row_b, 4)
    for _, target in in_z:
        send(deep_b.at[at_z], deep_b.at[at_z], deep_b_recv.at[at_z], target)
    across_z(zt, zt_in, zt_recv, t1, t1_in, t1_recv, 96)

    gathered(line_b, line_b_recv, in_line)
    means = group_totals(total(line_b, 8) * gains) / (FRAMES_CELLS * (C // GROUPS))
    inner = (grad_white - means[1:2] - whitened * means[0:1]) * inv
    grad_latents[...] = (cot[...].astype(F32) + inner).astype(BF16)
    store(grad_latents, latents_hbm)

    at_last(zs, zs_in, zs_recv, s_out, s_hbm)
    for o, _ in in_z:
        receive(deep_b.at[o], deep_b_recv.at[o])
    norm_out[...] = total(deep_b, 16) * scale
    store(norm_out, norm_hbm)
    at_last(zt, zt_in, zt_recv, t_out, t_hbm)
    for copy in stores:
        copy.wait()
    for copy in pending:
        copy.wait_send()


MAIN_OUTS = (
    ((ROWS, C), BF16), ((ROWS, C), BF16), ((4, 384), F32), ((4, 128), F32), ((2, C), F32),
)


def main(lat, cot, ws, wt, gain, bias):
    hbm = pl.BlockSpec(memory_space=pltpu.HBM)
    dma = pltpu.SemaphoreType.DMA
    V = pltpu.VMEM
    return pl.pallas_call(
        main_kernel,
        name="main",
        out_shape=[jax.ShapeDtypeStruct(*shape) for shape in MAIN_OUTS],
        in_specs=[hbm] * 6,
        out_specs=[hbm] * 5,
        scratch_shapes=[V(*shape) for shape in MAIN_OUTS]
        + [
            V((6, ROWS, C), BF16), V((1, C), F32), V((1, C), F32),
            V((NZH, NX, 36, 8, C), BF16), V((NZH, NX, 12, 8, C), BF16),
            V((8, 2, C), F32), V((8, 2, C), F32), V((8, 2, C), F32), V((8, 2, C), F32),
            V((NX, 2, C), F32), V((16, 2, C), F32),
            V((9 * C, C), BF16), V((3 * C, C), BF16),
            V((3 * ROWS, 9 * C), BF16), V((3 * ROWS, C), BF16), V((2 * ROWS, 3 * C), BF16),
            V((2 * ROWS, C), BF16), V((ROWS, 9 * C), BF16), V((HALF, 2 * ROWS), BF16),
            V((16, 32, S_WIN), BF16), V((16, 32, S_WIN), BF16),
            V((16, 32, T_WIN), BF16), V((16, 32, T_WIN), BF16),
            V((16, 4, 384), BF16), V((16, 4, 384), BF16),
            V((16, 4, 128), BF16), V((16, 4, 128), BF16),
            dma((6,)), dma((5,)), dma((SENDS,)),
            dma((8,)), dma((8,)), dma((8,)), dma((8,)), dma((4,)), dma((16,)),
            dma((2,)), dma((1,)), dma((1,)), dma((4,)), dma((1,)), dma((16,)),
            dma((4,)), dma((1,)), dma((16,)), dma((4,)), dma((1,)),
            dma((16,)), dma((16,)), dma((16,)), dma((16,)),
        ],
        compiler_params=pltpu.CompilerParams(
            collective_id=1, has_side_effects=True, vmem_limit_bytes=VMEM_BYTES
        ),
    )(lat, cot, ws, wt, gain, bias)


def finish_kernel(
    main_out, main_latents, main_s, main_t, main_norms,
    out_hbm, latents_hbm, spatial_hbm, temporal_hbm, norm_hbm,
    block_out, grad_latents, sums_s, sums_t, norms, spatial, temporal, norm,
    load_sem, store_sem,
):
    wide = lax.axis_index("wide")
    loads = [
        pltpu.make_async_copy(source, target, load_sem.at[k])
        for k, (source, target) in enumerate(
            (
                (main_norms, norms),
                (main_s, sums_s),
                (main_t, sums_t),
                (main_out, block_out),
                (main_latents, grad_latents),
            )
        )
    ]
    for copy in loads:
        copy.start()
    loads[0].wait()
    lane = lax.broadcasted_iota(jnp.int32, (2, C), 1)
    for k in range(4):
        norm[:, k : k + 1] = jnp.sum(
            jnp.where(lane == 4 * wide + k, norms[...], 0.0), axis=1, keepdims=True
        )
    loads[1].wait()
    spatial[...] = sums_s[:, :288]
    loads[2].wait()
    temporal[...] = sums_t[:, :96]
    loads[3].wait()
    loads[4].wait()
    stores = [
        pltpu.make_async_copy(source, target, store_sem.at[k])
        for k, (source, target) in enumerate(
            (
                (block_out, out_hbm),
                (grad_latents, latents_hbm),
                (spatial, spatial_hbm),
                (temporal, temporal_hbm),
                (norm, norm_hbm),
            )
        )
    ]
    for copy in stores:
        copy.start()
    for copy in stores:
        copy.wait()


def finish(*parts):
    hbm = pl.BlockSpec(memory_space=pltpu.HBM)
    dma = pltpu.SemaphoreType.DMA
    last = [((4, 288), F32), ((4, 96), F32), ((2, 4), F32)]
    return pl.pallas_call(
        finish_kernel,
        name="finish",
        out_shape=[jax.ShapeDtypeStruct(*shape) for shape in list(MAIN_OUTS[:2]) + last],
        in_specs=[hbm] * 5,
        out_specs=[hbm] * 5,
        scratch_shapes=[pltpu.VMEM(*shape) for shape in list(MAIN_OUTS) + last]
        + [dma((5,)), dma((5,))],
        compiler_params=pltpu.CompilerParams(vmem_limit_bytes=VMEM_BYTES),
    )(*parts)


def local(latents, cotangent, norm_gain, norm_bias, w_spatial, w_temporal):
    block_out, grad_latents, spatial, temporal, norm = finish(
        *main(
            latents.reshape(ROWS, C),
            cotangent.reshape(ROWS, C),
            w_spatial.reshape(36, 8, C),
            w_temporal.reshape(12, 8, C),
            norm_gain.reshape(1, C),
            norm_bias.reshape(1, C),
        )
    )
    return (
        block_out.reshape(latents.shape),
        grad_latents.reshape(latents.shape),
        spatial.T,
        temporal.T,
        norm,
    )


def solution(mesh):
    return jax.shard_map(
        local,
        mesh=mesh,
        in_specs=(
            P("dp", "wide", None, None, None),
            P("dp", "wide", None, None, None),
            P(),
            P(),
            P("dp", None),
            P("dp", None),
        ),
        out_specs=(
            P("dp", "wide", None, None, None),
            P("dp", "wide", None, None, None),
            P("dp", "wide"),
            P("dp", "wide"),
            P(None, "wide"),
        ),
        check_vma=False,
    )
```

time: 62.7 us -> 57.7 us (0.920)
  the two profiles are of different devices: /device:TPU:2 before, /device:TPU:1 now
where the time goes in v3:
time: 57.7 us; the launch traced here: 57.6 us
  Pallas kernels  56.9 us (99%)
  between operations  0.64 us (1%)
    pallas_call x1, Pallas kernels, main(): pl.pallas_call(main_kernel, name='main', out_shape=[jax.ShapeDtypeStruct(...  55.1 us
    pallas_call x1, Pallas kernels, finish(): pl.pallas_call(finish_kernel, name='finish', out_shape=[jax.ShapeDtypeStr...  1.78 us

profile of v3, /device:TPU:1, one launch (start us, length us, event | category | flops | bytes accessed | tf_op | source)
XLA Modules:
  0.0 57.6 jit_solution(13871084524463042660)
XLA Ops:
  0.6 55.1 %main.1 = (bf16[256,256]{1,0:T(8,128)(2,1)}, bf16[256,256]{1,0:T(8,128)(2,1)}, f32[4,384]{1,0:T(4,128)}, f32[4,128]{1,0:T(4,128)}, f32[2,256]{1,0:T(2,128)}) custom-call(bf16[256,256]{1,0:T(8,128)(2,1)} %bitcast.11, bf16[256,256]{1,0:T(8,128)(2,1)} %bitcast.12, bf16[36,8,256]{2,1,0:T(8,128)(2,1)} %bitcast.10, bf16[12,8,256]{2,1,0:T(8,128)(2,1)} %bitcast.13, ...), custom_call_target="tpu_custom_call" | custom-call | tf_op jit(solution)/shard_map/main/pallas_call | solution.py:444
  55.8 1.8 %finish.1 = (bf16[256,256]{1,0:T(8,128)(2,1)}, bf16[256,256]{1,0:T(8,128)(2,1)}, f32[4,288]{1,0:T(4,128)}, f32[4,96]{1,0:T(4,128)}, f32[2,4]{1,0:T(2,128)}) custom-call(bf16[256,256]{1,0:T(8,128)(2,1)} %get-tuple-element.15.main_out, bf16[256,256]{1,0:T(8,128)(2,1)} %get-tuple-element.16.main_latents, f32[4,384]{1,0:T(4,128)} %get-tuple-element.17.main_s, ...), custom_call_target="tpu_custom_call" | custom-call | tf_op jit(solution)/shard_map/finish/pallas_call | solution.py:530

commit v4 on v3

--- a/solution.py
+++ b/solution.py
@@ -17,8 +17,6 @@
 COLS = 16
 ROWS = 256
 NX, NZH, NY, NZL, NC = 4, 2, 4, 8, 2
-S_TILE = (0, 4, 9, 13)
-T_TILE = (0, 1, 3, 4)
 S_WIN = 5 * 128
 T_WIN = 2 * 128
 HALF = 128
@@ -143,18 +141,17 @@
 
 
 SENDS = 160
-VMEM_BYTES = 62 << 20
+VMEM_BYTES = 40 << 20
 
 
 def main_kernel(
     lat_hbm, cot_hbm, ws_hbm, wt_hbm, gain_hbm, bias_hbm,
-    out_hbm, latents_hbm, s_hbm, t_hbm, norm_hbm,
     block_out, grad_latents, s_out, t_out, norm_out,
     frames, gain, bias, wsp, wtm,
     plane, line, plane_b, line_b, row_b, deep_b,
-    w_sp, w_tm, windows, spatial, mixed, grad_act, adjoint, cot_t,
+    windows, spatial, mixed, grad_act, adjoint, cot_t,
     s1, s1_in, t1, t1_in, zs, zs_in, zt, zt_in,
-    local_sem, store_sem, send_sem,
+    local_sem, send_sem,
     plane_recv, line_recv, plane_b_recv, line_b_recv, row_b_recv, deep_b_recv,
     mate_recv, halo_recv, pass_recv, tx_recv, tz_recv, txy_recv,
     sx_recv, sz_recv, sxy_recv, c1_recv, c2_recv, s1_recv, t1_recv, zs_recv, zt_recv,
@@ -163,21 +160,6 @@
     wide, dp = lax.axis_index("wide"), lax.axis_index("dp")
     lat_at, cot_at, edge_out, edge_in = 1 + c, 3 + c, 3 - c, 5 - 5 * c
     lat, cot = frames.at[lat_at], frames.at[cot_at]
-    loads = [
-        pltpu.make_async_copy(source, target, local_sem.at[k])
-        for k, (source, target) in enumerate(
-            (
-                (lat_hbm, lat),
-                (wt_hbm, wtm.at[zh, x]),
-                (ws_hbm, wsp.at[zh, x]),
-                (cot_hbm, cot),
-                (gain_hbm, gain),
-                (bias_hbm, bias),
-            )
-        )
-    ]
-    for copy in loads:
-        copy.start()
     mine, in_plane = plane_peers(x, zh, y, zl, c)
     _, in_line = line_peers(x, zh, y, zl, c)
     others_x = [lax.rem(x + k, NX) for k in (1, 2, 3)]
@@ -197,18 +179,27 @@
         o = lax.rem(at_z + k, 16)
         in_z.append((o, device(x, lax.div(o, 8), y, lax.rem(o, 8), c)))
     arrived = greet(
-        [p for _, p in in_plane]
-        + [p for _, p in in_line]
+        [p for _, p in in_line]
+        + [to_far, ahead, behind]
         + [in_xy[k - 1][1] for k in range(4, 16)]
-        + [to_far, ahead, behind]
-    )
-
-    stores = []
-
-    def store(source, target):
-        copy = pltpu.make_async_copy(source, target, store_sem.at[len(stores)])
+        + [p for _, p in in_plane]
+    )
+
+    loads = [
+        pltpu.make_async_copy(source, target, local_sem.at[k])
+        for k, (source, target) in enumerate(
+            (
+                (lat_hbm, lat),
+                (wt_hbm, wtm.at[pl.ds(12 * dp, 12)]),
+                (ws_hbm, wsp.at[pl.ds(36 * dp, 36)]),
+                (cot_hbm, cot),
+                (gain_hbm, gain),
+                (bias_hbm, bias),
+            )
+        )
+    ]
+    for copy in loads:
         copy.start()
-        stores.append(copy)
 
     pending = []
 
@@ -216,6 +207,13 @@
         copy = remote(ref, target, send_sem.at[len(pending)], recv, where)
         copy.start()
         pending.append(copy)
+
+    drained = [0]
+
+    def drain():
+        for copy in pending[drained[0] :]:
+            copy.wait_send()
+        drained[0] = len(pending)
 
     def receive(ref, recv):
         remote(ref, ref, send_sem.at[0], recv, to_c).wait_recv()
@@ -236,20 +234,30 @@
         copy.wait()
     arrived()
 
+    def t_shard(hi, at):
+        return wtm.at[pl.ds(12 * (2 * at + hi), 12)]
+
+    def t_piece(at, quarter):
+        return wtm.at[pl.ds(12 * (2 * at + 1 - zh) + 3 * quarter, 3)]
+
+    def s_shard(hi, at, lanes):
+        return wsp.at[pl.ds(36 * (2 * at + hi), 36), :, lanes]
+
+    def s_piece(at, quarter, lanes):
+        return wsp.at[pl.ds(36 * (2 * at + 1 - zh) + 9 * quarter, 9), :, lanes]
+
+    part = wtm.at[pl.ds(12 * dp + 3 * y, 3)]
+    send(part, part, tz_recv.at[0], to_far)
     exchange(plane, plane_recv, mine, in_plane)
     lanes = pl.ds(pl.multiple_of(c * HALF, HALF), HALF)
-    t_rows = pl.ds(y * 3, 3)
-    s_rows = pl.ds(y * 9, 9)
-    part = wtm.at[zh, x, t_rows]
-    send(part, part, tz_recv.at[0], to_far)
-    part = wsp.at[zh, x, s_rows, :, lanes]
+    part = wsp.at[pl.ds(36 * dp + 9 * y, 9), :, lanes]
     send(part, part, sz_recv.at[0], to_far)
     for target in to_x:
-        send(wtm.at[zh, x], wtm.at[zh, x], tx_recv.at[x], target)
+        send(t_shard(zh, x), t_shard(zh, x), tx_recv.at[x], target)
     send(lat, lat, mate_recv.at[0], to_c)
     send(cot, cot, mate_recv.at[1], to_c)
     send(frames.at[edge_out], frames.at[edge_in], halo_recv.at[0], edge_to)
-    part = wsp.at[zh, x, :, :, lanes]
+    part = s_shard(zh, x, lanes)
     for target in to_x:
         send(part, part, sx_recv.at[x], target)
 
@@ -257,18 +265,18 @@
     line[zl] = total(plane, 8)
     exchange(line, line_recv, zl, in_line)
 
-    part = wtm.at[1 - zh, x, t_rows]
+    part = t_piece(x, y)
     receive(part, tz_recv.at[0])
     for _, target, _, _ in in_xy:
         send(part, part, txy_recv.at[at_xy], target)
-    part = wsp.at[1 - zh, x, s_rows, :, lanes]
+    part = s_piece(x, y, lanes)
     receive(part, sz_recv.at[0])
     for _, target, _, _ in in_xy:
         send(part, part, sxy_recv.at[at_xy], target)
     receive(frames.at[edge_in], halo_recv.at[0])
     send(frames.at[edge_in], frames.at[edge_in], pass_recv.at[0], to_c)
     for o in others_x:
-        part = wsp.at[zh, o, :, :, lanes]
+        part = s_shard(zh, o, lanes)
         receive(part, sx_recv.at[o])
         send(part, part, c1_recv.at[o], to_c)
     receive(frames.at[2 - c], mate_recv.at[0])
@@ -297,50 +305,59 @@
     last = frames[5]
     later = jnp.where(wide < 62, last.astype(F32), 0.0).astype(BF16)
     for o in others_x:
-        receive(wtm.at[zh, o], tx_recv.at[o])
+        receive(t_shard(zh, o), tx_recv.at[o])
     for slot, _, ox, oy in in_xy:
-        receive(wtm.at[1 - zh, ox, pl.ds(oy * 3, 3)], txy_recv.at[slot])
-    for d in range(8):
-        w_tm[d * 96 : (d + 1) * 96, :] = wtm[d % 2, d // 2].reshape(96, C)
+        receive(t_piece(ox, oy), txy_recv.at[slot])
     held = jnp.concatenate([frames[3], frames[4], later], axis=0)
     running = jnp.zeros((2 * ROWS, C), F32)
     for delay in range(3):
         start = delay * CELLS
         running = running + times_transpose(
-            held[start : start + 2 * ROWS], w_tm[delay * C : (delay + 1) * C, :]
+            held[start : start + 2 * ROWS], wtm[delay * 32 : (delay + 1) * 32].reshape(C, C)
         )
     grad_act[...] = running.astype(BF16)
     act_t = times_transpose(order, grad_act[...]).astype(BF16)
-    for o in range(NX):
-        start = S_TILE[o] * 128
-        piece = jnp.dot(
-            act_t, windows[ROWS:, start : start + S_WIN], preferred_element_type=F32
-        ).astype(BF16)
-        for p in range(NY):
-            s1[o * 4 + p] = piece[p * 32 : (p + 1) * 32, :]
-    for slot, target, _, _ in in_xy:
-        send(s1.at[slot], s1_in.at[at_xy], s1_recv.at[at_xy], target)
+
+    def scatter(left, right, slots, slots_in, recv, tiles, width, between):
+        for k in (1, 2, 3, 0):
+            o = lax.rem(x + k, NX)
+            start = pl.multiple_of(lax.div(tiles * o, 2) * 128, 128)
+            piece = jnp.dot(
+                left, right(pl.ds(start, width)), preferred_element_type=F32
+            ).astype(BF16)
+            for p in range(NY):
+                slots[o * 4 + p] = piece[p * 32 : (p + 1) * 32, :]
+            for slot, target, ox, _ in in_xy[max(4 * k - 1, 0) : 4 * k + 3]:
+                send(slots.at[slot], slots_in.at[at_xy], recv.at[at_xy], target)
+            between(k, o)
+
+    def pass_weights(k, o):
+        for slot, _, ox, oy in in_xy[max(4 * k - 1, 0) : 4 * k + 3]:
+            receive(s_piece(ox, oy, lanes), sxy_recv.at[slot])
+        part = s_shard(1 - zh, o, lanes)
+        send(part, part, c2_recv.at[o], to_c)
+
+    scatter(act_t, lambda at: windows[ROWS:, at], s1, s1_in, s1_recv, 9, S_WIN, lambda k, o: None)
 
     own_rows = pl.ds(pl.multiple_of(c * ROWS, ROWS), ROWS)
     fill_windows(adjoint, grad_act[own_rows, :].astype(F32), -1)
     _, normed = normed_of(frames[0])
     fill_windows(windows.at[0:ROWS, :], normed * jax.nn.sigmoid(normed), 1)
 
-    for slot, _, ox, oy in in_xy:
-        receive(wsp.at[1 - zh, ox, pl.ds(oy * 9, 9), :, lanes], sxy_recv.at[slot])
-    part = wsp.at[1 - zh, :, :, :, lanes]
-    send(part, part, c2_recv.at[0], to_c)
+    for k in (1, 2, 3, 0):
+        pass_weights(k, lax.rem(x + k, NX))
     other_lanes = pl.ds(pl.multiple_of((1 - c) * HALF, HALF), HALF)
     for o in others_x:
-        receive(wsp.at[zh, o, :, :, other_lanes], c1_recv.at[o])
-    receive(wsp.at[1 - zh, :, :, :, other_lanes], c2_recv.at[0])
-    for d in range(8):
-        w_sp[d * 288 : (d + 1) * 288, :] = wsp[d % 2, d // 2].reshape(288, C)
+        receive(s_shard(zh, o, other_lanes), c1_recv.at[o])
+    for o in range(NX):
+        receive(s_shard(1 - zh, o, other_lanes), c2_recv.at[o])
 
     running = jnp.zeros((ROWS, C), F32)
     for tap in range(9):
         taps = slice(tap * C, (tap + 1) * C)
-        running = running + times_transpose(adjoint[:, taps], w_sp[taps, :])
+        running = running + times_transpose(
+            adjoint[:, taps], wsp[tap * 32 : (tap + 1) * 32].reshape(C, C)
+        )
     whitened, normed = normed_of(lat[...])
     sigmoid = jax.nn.sigmoid(normed)
     grad_normed = running * (sigmoid * (1.0 + normed * (1.0 - sigmoid)))
@@ -349,24 +366,17 @@
     exchange(plane_b, plane_b_recv, mine, in_plane)
     grad_white = grad_normed * gains
 
-    conv = jnp.dot(windows[...], w_sp[...], preferred_element_type=F32)
+    conv = jnp.dot(windows[...], wsp[...].reshape(9 * C, C), preferred_element_type=F32)
     spatial[ROWS:, :] = conv[ROWS:].astype(BF16)
     spatial[:ROWS, :] = jnp.where(wide > 1, conv[:ROWS], 0.0).astype(BF16)
     for delay in range(3):
         start = (2 - delay) * CELLS
         mixed[:, delay * C : (delay + 1) * C] = spatial[start : start + 2 * ROWS, :]
-    for o in range(NX):
-        start = T_TILE[o] * 128
-        piece = jnp.dot(
-            cot_t[...], mixed[:, start : start + T_WIN], preferred_element_type=F32
-        ).astype(BF16)
-        for p in range(NY):
-            t1[o * 4 + p] = piece[p * 32 : (p + 1) * 32, :]
-    for slot, target, _, _ in in_xy:
-        send(t1.at[slot], t1_in.at[at_xy], t1_recv.at[at_xy], target)
-    temporal = jnp.dot(mixed[own_rows, :], w_tm[...], preferred_element_type=F32)
+    scatter(cot_t[...], lambda at: mixed[:, at], t1, t1_in, t1_recv, 3, T_WIN, lambda k, o: None)
+    temporal = jnp.dot(
+        mixed[own_rows, :], wtm[...].reshape(3 * C, C), preferred_element_type=F32
+    )
     block_out[...] = (lat[...].astype(F32) + temporal).astype(BF16)
-    store(block_out, out_hbm)
 
     gathered(plane_b, plane_b_recv, in_plane)
     sums_b = total(plane_b, 8)
@@ -379,10 +389,9 @@
     odd = lax.rem(x, 2)
 
     def across_z(slots, slots_in, recv, source, source_in, source_recv, width):
+        joined = source[at_xy].astype(F32)
         for slot, _, _, _ in in_xy:
             receive(source_in.at[slot], source_recv.at[slot])
-        joined = source[at_xy].astype(F32)
-        for slot, _, _, _ in in_xy:
             joined = joined + source_in[slot].astype(F32)
         for hi in range(NZH):
             at = width * hi
@@ -397,43 +406,38 @@
 
     scale = 1.0 / math.sqrt(131072)
 
-    def at_last(slots, slots_in, recv, out, out_hbm):
+    def at_last(slots, slots_in, recv, out):
+        result = slots[at_z].astype(F32)
         for o, _ in in_z:
             receive(slots_in.at[o], recv.at[o])
-        result = slots[at_z].astype(F32)
-        for o, _ in in_z:
             result = result + slots_in[o].astype(F32)
         out[...] = result * scale
-        store(out, out_hbm)
-
+
+    drain()
     across_z(zs, zs_in, zs_recv, s1, s1_in, s1_recv, 288)
+    across_z(zt, zt_in, zt_recv, t1, t1_in, t1_recv, 96)
     for o in others_x:
         receive(row_b.at[o], row_b_recv.at[o])
-    deep_b[at_z] = total(row_b, 4)
+    both = total(row_b, 4)
+    deep_b[at_z] = jnp.where(y < 2, both[:, :HALF], both[:, HALF:])
     for _, target in in_z:
         send(deep_b.at[at_z], deep_b.at[at_z], deep_b_recv.at[at_z], target)
-    across_z(zt, zt_in, zt_recv, t1, t1_in, t1_recv, 96)
 
     gathered(line_b, line_b_recv, in_line)
     means = group_totals(total(line_b, 8) * gains) / (FRAMES_CELLS * (C // GROUPS))
     inner = (grad_white - means[1:2] - whitened * means[0:1]) * inv
     grad_latents[...] = (cot[...].astype(F32) + inner).astype(BF16)
-    store(grad_latents, latents_hbm)
-
-    at_last(zs, zs_in, zs_recv, s_out, s_hbm)
+
+    at_last(zs, zs_in, zs_recv, s_out)
     for o, _ in in_z:
         receive(deep_b.at[o], deep_b_recv.at[o])
     norm_out[...] = total(deep_b, 16) * scale
-    store(norm_out, norm_hbm)
-    at_last(zt, zt_in, zt_recv, t_out, t_hbm)
-    for copy in stores:
-        copy.wait()
-    for copy in pending:
-        copy.wait_send()
+    at_last(zt, zt_in, zt_recv, t_out)
+    drain()
 
 
 MAIN_OUTS = (
-    ((ROWS, C), BF16), ((ROWS, C), BF16), ((4, 384), F32), ((4, 128), F32), ((2, C), F32),
+    ((ROWS, C), BF16), ((ROWS, C), BF16), ((4, 384), F32), ((4, 128), F32), ((2, HALF), F32),
 )
 
 
@@ -446,65 +450,36 @@
         name="main",
         out_shape=[jax.ShapeDtypeStruct(*shape) for shape in MAIN_OUTS],
         in_specs=[hbm] * 6,
-        out_specs=[hbm] * 5,
-        scratch_shapes=[V(*shape) for shape in MAIN_OUTS]
-        + [
+        out_specs=[pl.BlockSpec(memory_space=pltpu.VMEM)] * 5,
+        scratch_shapes=[
             V((6, ROWS, C), BF16), V((1, C), F32), V((1, C), F32),
-            V((NZH, NX, 36, 8, C), BF16), V((NZH, NX, 12, 8, C), BF16),
+            V((8 * 36, 8, C), BF16), V((8 * 12, 8, C), BF16),
             V((8, 2, C), F32), V((8, 2, C), F32), V((8, 2, C), F32), V((8, 2, C), F32),
-            V((NX, 2, C), F32), V((16, 2, C), F32),
-            V((9 * C, C), BF16), V((3 * C, C), BF16),
+            V((NX, 2, C), F32), V((16, 2, HALF), F32),
             V((3 * ROWS, 9 * C), BF16), V((3 * ROWS, C), BF16), V((2 * ROWS, 3 * C), BF16),
             V((2 * ROWS, C), BF16), V((ROWS, 9 * C), BF16), V((HALF, 2 * ROWS), BF16),
             V((16, 32, S_WIN), BF16), V((16, 32, S_WIN), BF16),
             V((16, 32, T_WIN), BF16), V((16, 32, T_WIN), BF16),
             V((16, 4, 384), BF16), V((16, 4, 384), BF16),
             V((16, 4, 128), BF16), V((16, 4, 128), BF16),
-            dma((6,)), dma((5,)), dma((SENDS,)),
+            dma((6,)), dma((SENDS,)),
             dma((8,)), dma((8,)), dma((8,)), dma((8,)), dma((4,)), dma((16,)),
             dma((2,)), dma((1,)), dma((1,)), dma((4,)), dma((1,)), dma((16,)),
-            dma((4,)), dma((1,)), dma((16,)), dma((4,)), dma((1,)),
+            dma((4,)), dma((1,)), dma((16,)), dma((4,)), dma((4,)),
             dma((16,)), dma((16,)), dma((16,)), dma((16,)),
         ],
         compiler_params=pltpu.CompilerParams(
             collective_id=1, has_side_effects=True, vmem_limit_bytes=VMEM_BYTES
         ),
-    )(lat, cot, ws, wt, gain, bias)
+    )(*[pltpu.with_memory_space_constraint(a, pltpu.HBM) for a in (lat, cot, ws, wt, gain, bias)])
 
 
 def finish_kernel(
-    main_out, main_latents, main_s, main_t, main_norms,
+    block_out, grad_latents, sums_s, sums_t, norms,
     out_hbm, latents_hbm, spatial_hbm, temporal_hbm, norm_hbm,
-    block_out, grad_latents, sums_s, sums_t, norms, spatial, temporal, norm,
-    load_sem, store_sem,
+    spatial, temporal, norm, store_sem,
 ):
     wide = lax.axis_index("wide")
-    loads = [
-        pltpu.make_async_copy(source, target, load_sem.at[k])
-        for k, (source, target) in enumerate(
-            (
-                (main_norms, norms),
-                (main_s, sums_s),
-                (main_t, sums_t),
-                (main_out, block_out),
-                (main_latents, grad_latents),
-            )
-        )
-    ]
-    for copy in loads:
-        copy.start()
-    loads[0].wait()
-    lane = lax.broadcasted_iota(jnp.int32, (2, C), 1)
-    for k in range(4):
-        norm[:, k : k + 1] = jnp.sum(
-            jnp.where(lane == 4 * wide + k, norms[...], 0.0), axis=1, keepdims=True
-        )
-    loads[1].wait()
-    spatial[...] = sums_s[:, :288]
-    loads[2].wait()
-    temporal[...] = sums_t[:, :96]
-    loads[3].wait()
-    loads[4].wait()
     stores = [
         pltpu.make_async_copy(source, target, store_sem.at[k])
         for k, (source, target) in enumerate(
@@ -517,8 +492,18 @@
             )
         )
     ]
-    for copy in stores:
-        copy.start()
+    stores[0].start()
+    stores[1].start()
+    spatial[...] = sums_s[:, :288]
+    stores[2].start()
+    temporal[...] = sums_t[:, :96]
+    stores[3].start()
+    lane = lax.broadcasted_iota(jnp.int32, (2, HALF), 1)
+    for k in range(4):
+        norm[:, k : k + 1] = jnp.sum(
+            jnp.where(lane == lax.rem(4 * wide, HALF) + k, norms[...], 0.0), axis=1, keepdims=True
+        )
+    stores[4].start()
     for copy in stores:
         copy.wait()
 
@@ -531,11 +516,10 @@
         finish_kernel,
         name="finish",
         out_shape=[jax.ShapeDtypeStruct(*shape) for shape in list(MAIN_OUTS[:2]) + last],
-        in_specs=[hbm] * 5,
+        in_specs=[pl.BlockSpec(memory_space=pltpu.VMEM)] * 5,
         out_specs=[hbm] * 5,
-        scratch_shapes=[pltpu.VMEM(*shape) for shape in list(MAIN_OUTS) + last]
-        + [dma((5,)), dma((5,))],
-        compiler_params=pltpu.CompilerParams(vmem_limit_bytes=VMEM_BYTES),
+        scratch_shapes=[pltpu.VMEM(*shape) for shape in last] + [dma((5,))],
+        compiler_params=pltpu.CompilerParams(vmem_limit_bytes=2 << 20),
     )(*parts)
 
 

time: 57.7 us -> 55.1 us (0.955)
  Pallas kernels: 56.9 us -> 54.4 us
    pallas_call x1, Pallas kernels: 55.1 us -> 53.6 us  [main(): pl.pallas_call(main_kernel, name='main', out_shape=[jax.ShapeDtypeStruct(...]
    pallas_call x1, Pallas kernels: 1.78 us -> 0.75 us  [finish(): pl.pallas_call(finish_kernel, name='finish', out_shape=[jax.ShapeDtypeStr...]
where the time goes in v4:
time: 55.1 us; the launch traced here: 55 us
  Pallas kernels  54.4 us (99%)
  between operations  0.64 us (1%)
    pallas_call x1, Pallas kernels, main(): pl.pallas_call(main_kernel, name='main', out_shape=[jax.ShapeDtypeStruct(...  53.6 us

profile of v4, /device:TPU:1, one launch (start us, length us, event | category | flops | bytes accessed | tf_op | source)
XLA Modules:
  0.0 55.0 jit_solution(2015627380414880616)
XLA Ops:
  0.6 53.6 %main.1 = (bf16[256,256]{1,0:T(8,128)(2,1)S(1)}, bf16[256,256]{1,0:T(8,128)(2,1)S(1)}, f32[4,384]{1,0:T(4,128)S(1)}, f32[4,128]{1,0:T(4,128)S(1)}, f32[2,128]{1,0:T(2,128)S(1)}) custom-call(bf16[256,256]{1,0:T(8,128)(2,1)} %bitcast.11, bf16[256,256]{1,0:T(8,128)(2,1)} %bitcast.12, bf16[36,8,256]{2,1,0:T(8,128)(2,1)} %bitcast.10, ...), custom_call_target="tpu_custom_call" | custom-call | tf_op jit(solution)/shard_map/main/pallas_call | solution.py:448
  54.3 0.8 %finish.1 = (bf16[256,256]{1,0:T(8,128)(2,1)}, bf16[256,256]{1,0:T(8,128)(2,1)}, f32[4,288]{1,0:T(4,128)}, f32[4,96]{1,0:T(4,128)}, f32[2,4]{1,0:T(2,128)}) custom-call(bf16[256,256]{1,0:T(8,128)(2,1)S(1)} %get-tuple-element.15.block_out, bf16[256,256]{1,0:T(8,128)(2,1)S(1)} %get-tuple-element.16.grad_latents, f32[4,384]{1,0:T(4,128)S(1)} %get-tuple-element.17.sums_s, ...), custom_call_target="tpu_custom_call" | custom-call | tf_op jit(solution)/shard_map/finish/pallas_call | solution.py:515

commit v5 on v4

--- a/solution.py
+++ b/solution.py
@@ -17,8 +17,7 @@
 COLS = 16
 ROWS = 256
 NX, NZH, NY, NZL, NC = 4, 2, 4, 8, 2
-S_WIN = 5 * 128
-T_WIN = 2 * 128
+S_TILES, T_TILES = 4, 1
 HALF = 128
 
 
@@ -318,18 +317,35 @@
     grad_act[...] = running.astype(BF16)
     act_t = times_transpose(order, grad_act[...]).astype(BF16)
 
-    def scatter(left, right, slots, slots_in, recv, tiles, width, between):
+    def scatter(left, right, slots, slots_in, recv, tiles):
         for k in (1, 2, 3, 0):
             o = lax.rem(x + k, NX)
-            start = pl.multiple_of(lax.div(tiles * o, 2) * 128, 128)
-            piece = jnp.dot(
-                left, right(pl.ds(start, width)), preferred_element_type=F32
+            odd_o = lax.rem(o, 2)
+            first = lax.div((2 * tiles + 1) * o + 1, 2)
+            whole = jnp.dot(
+                left,
+                right(pl.ds(pl.multiple_of(first * 128, 128), tiles * 128)),
+                preferred_element_type=F32,
             ).astype(BF16)
+            at_half = first + tiles - (tiles + 1) * odd_o
+            half = jnp.dot(
+                left, right(pl.ds(pl.multiple_of(at_half * 128, 128), 128)), preferred_element_type=F32
+            )
+            turned = pltpu.roll(half, 64, 1)
+            low = jnp.where(odd_o == 1, turned, half)
+            high = jnp.where(odd_o == 1, half, turned)
+            left_half = lax.broadcasted_iota(jnp.int32, (16, 128), 1) < 64
             for p in range(NY):
-                slots[o * 4 + p] = piece[p * 32 : (p + 1) * 32, :]
-            for slot, target, ox, _ in in_xy[max(4 * k - 1, 0) : 4 * k + 3]:
+                slot = o * 4 + p
+                for tile in range(tiles):
+                    slots[slot, tile * 32 : (tile + 1) * 32, :] = whole[
+                        p * 32 : (p + 1) * 32, tile * 128 : (tile + 1) * 128
+                    ]
+                slots[slot, tiles * 32 :, :] = jnp.where(
+                    left_half, low[p * 32 : p * 32 + 16], high[p * 32 + 16 : (p + 1) * 32]
+                ).astype(BF16)
+            for slot, target, _, _ in in_xy[max(4 * k - 1, 0) : 4 * k + 3]:
                 send(slots.at[slot], slots_in.at[at_xy], recv.at[at_xy], target)
-            between(k, o)
 
     def pass_weights(k, o):
         for slot, _, ox, oy in in_xy[max(4 * k - 1, 0) : 4 * k + 3]:
@@ -337,7 +353,7 @@
         part = s_shard(1 - zh, o, lanes)
         send(part, part, c2_recv.at[o], to_c)
 
-    scatter(act_t, lambda at: windows[ROWS:, at], s1, s1_in, s1_recv, 9, S_WIN, lambda k, o: None)
+    scatter(act_t, lambda at: windows[ROWS:, at], s1, s1_in, s1_recv, S_TILES)
 
     own_rows = pl.ds(pl.multiple_of(c * ROWS, ROWS), ROWS)
     fill_windows(adjoint, grad_act[own_rows, :].astype(F32), -1)
@@ -372,12 +388,7 @@
     for delay in range(3):
         start = (2 - delay) * CELLS
         mixed[:, delay * C : (delay + 1) * C] = spatial[start : start + 2 * ROWS, :]
-    scatter(cot_t[...], lambda at: mixed[:, at], t1, t1_in, t1_recv, 3, T_WIN, lambda k, o: None)
-    temporal = jnp.dot(
-        mixed[own_rows, :], wtm[...].reshape(3 * C, C), preferred_element_type=F32
-    )
-    block_out[...] = (lat[...].astype(F32) + temporal).astype(BF16)
-
+    scatter(cot_t[...], lambda at: mixed[:, at], t1, t1_in, t1_recv, T_TILES)
     gathered(plane_b, plane_b_recv, in_plane)
     sums_b = total(plane_b, 8)
     line_b[zl] = sums_b
@@ -385,19 +396,29 @@
     exchange(line_b, line_b_recv, zl, in_line)
     for target in to_x:
         send(row_b.at[x], row_b.at[x], row_b_recv.at[x], target)
+    temporal = jnp.dot(
+        mixed[own_rows, :], wtm[...].reshape(3 * C, C), preferred_element_type=F32
+    )
+    block_out[...] = (lat[...].astype(F32) + temporal).astype(BF16)
+
 
     odd = lax.rem(x, 2)
 
-    def across_z(slots, slots_in, recv, source, source_in, source_recv, width):
+    def across_z(slots, slots_in, recv, source, source_in, source_recv, tiles, width):
         joined = source[at_xy].astype(F32)
         for slot, _, _, _ in in_xy:
             receive(source_in.at[slot], source_recv.at[slot])
             joined = joined + source_in[slot].astype(F32)
+        whole = [joined[tile * 32 : (tile + 1) * 32] for tile in range(tiles)]
+        fold = joined[tiles * 32 :]
+        half = jnp.concatenate([fold[:, :64], fold[:, 64:]], axis=0)
+        columns = jnp.where(
+            odd == 1,
+            jnp.concatenate([half] + whole, axis=1),
+            jnp.concatenate(whole + [half], axis=1),
+        )
         for hi in range(NZH):
-            at = width * hi
-            mid = jnp.where(
-                odd == 1, joined[:, at + 64 : at + 64 + width], joined[:, at : at + width]
-            )
+            mid = columns[:, width * hi : width * (hi + 1)]
             for q in range(8):
                 slots[hi * 8 + q, :, 0:width] = mid[q * 4 : (q + 1) * 4].astype(BF16)
                 slots[hi * 8 + q, :, width:] = jnp.zeros((4, slots.shape[2] - width), BF16)
@@ -413,9 +434,8 @@
             result = result + slots_in[o].astype(F32)
         out[...] = result * scale
 
-    drain()
-    across_z(zs, zs_in, zs_recv, s1, s1_in, s1_recv, 288)
-    across_z(zt, zt_in, zt_recv, t1, t1_in, t1_recv, 96)
+    across_z(zs, zs_in, zs_recv, s1, s1_in, s1_recv, S_TILES, 288)
+    across_z(zt, zt_in, zt_recv, t1, t1_in, t1_recv, T_TILES, 96)
     for o in others_x:
         receive(row_b.at[o], row_b_recv.at[o])
     both = total(row_b, 4)
@@ -423,6 +443,7 @@
     for _, target in in_z:
         send(deep_b.at[at_z], deep_b.at[at_z], deep_b_recv.at[at_z], target)
 
+    drain()
     gathered(line_b, line_b_recv, in_line)
     means = group_totals(total(line_b, 8) * gains) / (FRAMES_CELLS * (C // GROUPS))
     inner = (grad_white - means[1:2] - whitened * means[0:1]) * inv
@@ -458,8 +479,8 @@
             V((NX, 2, C), F32), V((16, 2, HALF), F32),
             V((3 * ROWS, 9 * C), BF16), V((3 * ROWS, C), BF16), V((2 * ROWS, 3 * C), BF16),
             V((2 * ROWS, C), BF16), V((ROWS, 9 * C), BF16), V((HALF, 2 * ROWS), BF16),
-            V((16, 32, S_WIN), BF16), V((16, 32, S_WIN), BF16),
-            V((16, 32, T_WIN), BF16), V((16, 32, T_WIN), BF16),
+            V((16, 32 * S_TILES + 16, 128), BF16), V((16, 32 * S_TILES + 16, 128), BF16),
+            V((16, 32 * T_TILES + 16, 128), BF16), V((16, 32 * T_TILES + 16, 128), BF16),
             V((16, 4, 384), BF16), V((16, 4, 384), BF16),
             V((16, 4, 128), BF16), V((16, 4, 128), BF16),
             dma((6,)), dma((SENDS,)),

time: 55.1 us -> 54.6 us (level)
  the two profiles are of different devices: /device:TPU:1 before, /device:TPU:8 now
where the time goes in v5:
time: 54.6 us; the launch traced here: 54.5 us
  Pallas kernels  53.8 us (99%)
  between operations  0.64 us (1%)
    pallas_call x1, Pallas kernels, main(): pl.pallas_call(main_kernel, name='main', out_shape=[jax.ShapeDtypeStruct(...  53.1 us

profile of v5, /device:TPU:8, one launch (start us, length us, event | category | flops | bytes accessed | tf_op | source)
XLA Modules:
  0.0 54.5 jit_solution(5415640697040131289)
XLA Ops:
  0.6 53.1 %main.1 = (bf16[256,256]{1,0:T(8,128)(2,1)S(1)}, bf16[256,256]{1,0:T(8,128)(2,1)S(1)}, f32[4,384]{1,0:T(4,128)S(1)}, f32[4,128]{1,0:T(4,128)S(1)}, f32[2,128]{1,0:T(2,128)S(1)}) custom-call(bf16[256,256]{1,0:T(8,128)(2,1)} %bitcast.11, bf16[256,256]{1,0:T(8,128)(2,1)} %bitcast.12, bf16[36,8,256]{2,1,0:T(8,128)(2,1)} %bitcast.10, ...), custom_call_target="tpu_custom_call" | custom-call | tf_op jit(solution)/shard_map/main/pallas_call | solution.py:469
  53.7 0.8 %finish.1 = (bf16[256,256]{1,0:T(8,128)(2,1)}, bf16[256,256]{1,0:T(8,128)(2,1)}, f32[4,288]{1,0:T(4,128)}, f32[4,96]{1,0:T(4,128)}, f32[2,4]{1,0:T(2,128)}) custom-call(bf16[256,256]{1,0:T(8,128)(2,1)S(1)} %get-tuple-element.15.block_out, bf16[256,256]{1,0:T(8,128)(2,1)S(1)} %get-tuple-element.16.grad_latents, f32[4,384]{1,0:T(4,128)S(1)} %get-tuple-element.17.sums_s, ...), custom_call_target="tpu_custom_call" | custom-call | tf_op jit(solution)/shard_map/finish/pallas_call | solution.py:536

commit v6 on v5

--- a/solution.py
+++ b/solution.py
@@ -169,12 +169,14 @@
     edge_to = (dp, lax.rem(wide + 62 + 4 * c, 64))
     at_xy = x * 4 + y
     in_xy = []
-    for k in range(1, 16):
-        ox, oy = lax.rem(x + k // 4, NX), lax.rem(y + k % 4, NY)
-        in_xy.append((ox * 4 + oy, device(ox, zh, oy, zl, c), ox, oy))
+    for kx in range(NX):
+        for ky in (2, 1, 3, 0):
+            if kx + ky:
+                ox, oy = lax.rem(x + kx, NX), lax.rem(y + ky, NY)
+                in_xy.append((ox * 4 + oy, device(ox, zh, oy, zl, c), ox, oy))
     at_z = zh * 8 + zl
     in_z = []
-    for k in range(1, 16):
+    for k in (8, 7, 9, 6, 10, 5, 11, 4, 12, 3, 13, 2, 14, 1, 15):
         o = lax.rem(at_z + k, 16)
         in_z.append((o, device(x, lax.div(o, 8), y, lax.rem(o, 8), c)))
     arrived = greet(
@@ -318,7 +320,7 @@
     act_t = times_transpose(order, grad_act[...]).astype(BF16)
 
     def scatter(left, right, slots, slots_in, recv, tiles):
-        for k in (1, 2, 3, 0):
+        for k in (2, 0, 1, 3):
             o = lax.rem(x + k, NX)
             odd_o = lax.rem(o, 2)
             first = lax.div((2 * tiles + 1) * o + 1, 2)

time: 54.6 us -> 53.2 us (0.974)
  the two profiles are of different devices: /device:TPU:8 before, /device:TPU:1 now
where the time goes in v6:
time: 53.2 us; the launch traced here: 52.8 us
  Pallas kernels  52.2 us (98%)
  between operations  0.64 us (1%)
    pallas_call x1, Pallas kernels, main(): pl.pallas_call(main_kernel, name='main', out_shape=[jax.ShapeDtypeStruct(...  51.4 us

profile of v6, /device:TPU:1, one launch (start us, length us, event | category | flops | bytes accessed | tf_op | source)
XLA Modules:
  0.0 52.8 jit_solution(9843784505894217132)
XLA Ops:
  0.6 51.4 %main.1 = (bf16[256,256]{1,0:T(8,128)(2,1)S(1)}, bf16[256,256]{1,0:T(8,128)(2,1)S(1)}, f32[4,384]{1,0:T(4,128)S(1)}, f32[4,128]{1,0:T(4,128)S(1)}, f32[2,128]{1,0:T(2,128)S(1)}) custom-call(bf16[256,256]{1,0:T(8,128)(2,1)} %bitcast.11, bf16[256,256]{1,0:T(8,128)(2,1)} %bitcast.12, bf16[36,8,256]{2,1,0:T(8,128)(2,1)} %bitcast.10, ...), custom_call_target="tpu_custom_call" | custom-call | tf_op jit(solution)/shard_map/main/pallas_call | solution.py:471
  52.0 0.8 %finish.1 = (bf16[256,256]{1,0:T(8,128)(2,1)}, bf16[256,256]{1,0:T(8,128)(2,1)}, f32[4,288]{1,0:T(4,128)}, f32[4,96]{1,0:T(4,128)}, f32[2,4]{1,0:T(2,128)}) custom-call(bf16[256,256]{1,0:T(8,128)(2,1)S(1)} %get-tuple-element.15.block_out, bf16[256,256]{1,0:T(8,128)(2,1)S(1)} %get-tuple-element.16.grad_latents, f32[4,384]{1,0:T(4,128)S(1)} %get-tuple-element.17.sums_s, ...), custom_call_target="tpu_custom_call" | custom-call | tf_op jit(solution)/shard_map/finish/pallas_call | solution.py:538

commit v7 on v6

--- a/solution.py
+++ b/solution.py
@@ -66,7 +66,7 @@
 def line_peers(x, zh, y, zl, c):
     peers = []
     for k in range(1, 8):
-        other = lax.rem(zl + k, 8)
+        other = lax.rem(zl + k + (1 - lax.div(zl, 4)) * (8 - 2 * k), 8)
         peers.append((other, device(x, zh, y, other, c)))
     return zl, peers
 

time: 53.2 us -> 53.2 us (level)
  no operation moved by 1% of the time
where the time goes in v7:
time: 53.2 us; the launch traced here: 52.8 us
  Pallas kernels  52.1 us (98%)
  between operations  0.64 us (1%)
    pallas_call x1, Pallas kernels, main(): pl.pallas_call(main_kernel, name='main', out_shape=[jax.ShapeDtypeStruct(...  51.4 us

profile of v7, /device:TPU:1, one launch (start us, length us, event | category | flops | bytes accessed | tf_op | source)
XLA Modules:
  0.0 52.8 jit_solution(16114717676628160067)
XLA Ops:
  0.6 51.4 %main.1 = (bf16[256,256]{1,0:T(8,128)(2,1)S(1)}, bf16[256,256]{1,0:T(8,128)(2,1)S(1)}, f32[4,384]{1,0:T(4,128)S(1)}, f32[4,128]{1,0:T(4,128)S(1)}, f32[2,128]{1,0:T(2,128)S(1)}) custom-call(bf16[256,256]{1,0:T(8,128)(2,1)} %bitcast.11, bf16[256,256]{1,0:T(8,128)(2,1)} %bitcast.12, bf16[36,8,256]{2,1,0:T(8,128)(2,1)} %bitcast.10, ...), custom_call_target="tpu_custom_call" | custom-call | tf_op jit(solution)/shard_map/main/pallas_call | solution.py:471
  52.0 0.8 %finish.1 = (bf16[256,256]{1,0:T(8,128)(2,1)}, bf16[256,256]{1,0:T(8,128)(2,1)}, f32[4,288]{1,0:T(4,128)}, f32[4,96]{1,0:T(4,128)}, f32[2,4]{1,0:T(2,128)}) custom-call(bf16[256,256]{1,0:T(8,128)(2,1)S(1)} %get-tuple-element.15.block_out, bf16[256,256]{1,0:T(8,128)(2,1)S(1)} %get-tuple-element.16.grad_latents, f32[4,384]{1,0:T(4,128)S(1)} %get-tuple-element.17.sums_s, ...), custom_call_target="tpu_custom_call" | custom-call | tf_op jit(solution)/shard_map/finish/pallas_call | solution.py:538
